TPU v7x, 32 devices: a whole 2x2x4 slice. The times are simulated.
32 devices in a mesh: dp: 8 (over z, y), mp: 4 (over x, core).
Axes of the slice: x: 2, y: 2, z: 4, core: 2. Of those that a mesh axis runs over, the one named last changes fastest.
Arguments:
- frames: bfloat16 [4, 4608, 768], P(None, ('dp', 'mp')), may hold values from -6 to 6
- clip_ids: int32 [4, 4608], replicated, may hold values from 0 to 5, never falling along the last dimension, each value on 1 to 1500 neighbouring positions
- w_qkv: bfloat16 [768, 3, 768], P('dp', None, 'mp'), may hold values from -0.21875 to 0.21875
- b_qv: bfloat16 [2, 4, 192], P(None, 'mp', 'dp'), may hold values from -3 to 3
- w_out: bfloat16 [768, 768], P('mp', 'dp'), may hold values from -2.5 to 2.5
- w_up: bfloat16 [768, 3072], P('dp', 'mp'), may hold values from -0.21875 to 0.21875
- b_up: bfloat16 [4, 768], P('mp', 'dp'), may hold values from -3 to 3
- w_down: bfloat16 [3072, 768], P('mp', 'dp'), may hold values from -0.109375 to 0.109375
- gains: bfloat16 [2, 768], P(None, ('dp', 'mp')), may hold values from 0.099609375 to 1.8984375
- biases: bfloat16 [4, 768], P(None, ('dp', 'mp')), may hold values from -3 to 3
- cotangent: bfloat16 [4, 4608, 768], P(None, ('dp', 'mp')), may hold values from -6 to 6
Outputs:
- output: bfloat16 [4, 4608, 768], P(None, ('dp', 'mp'))
- frames_grad: bfloat16 [4, 4608, 768], P(None, ('dp', 'mp'))
- grad_qkv: float32 [768, 3, 768], P('dp', None, 'mp')
- grad_bqv: float32 [2, 4, 192], P(None, 'mp', 'dp')
- grad_out: float32 [768, 768], P('mp', 'dp')
- grad_up: float32 [768, 3072], P('dp', 'mp')
- grad_bup: float32 [4, 768], P('mp', 'dp')
- grad_down: float32 [3072, 768], P('mp', 'dp')
- grad_gains: float32 [2, 768], P(None, ('dp', 'mp'))
- grad_biases: float32 [4, 768], P(None, ('dp', 'mp'))
Inputs may be any that keep to these rules, and one draw needn't show every extreme that they name: `clip_ids`: in each micro-batch the clip ids never fall along the frames; each clip is a run of 1 to 1500 frames, and one clip of each micro-batch has exactly 1500.
All inputs are finite; a program needn't handle non-finite values.
Results may differ from a plain program's by a relative error of at most 0.017.
Values may be sent and summed in bfloat16 or wider, within the bound.
No kernel may reach another device: no remote copies, remote signals or barrier semaphores. Data moves between devices by JAX's collectives and lax.ppermute only.
A program may use at most 192 MiB of HBM per device.

v0:
```python
import jax
import jax.numpy as jnp
from jax import lax
from jax.sharding import PartitionSpec as P

D = 768
HD = 64
CLIP = 1500


epsilon = 1e-05
masked_score = -1e30


def passed_along(array, axis, by):
    peers = lax.axis_size(axis)
    pairs = [(i, i + by) for i in range(peers) if 0 <= i + by < peers]
    return lax.ppermute(array, axis, pairs)


def shortened(array):
    return jax.tree.map(lambda a: a.astype(jnp.bfloat16) if a.dtype == jnp.float32 else a, array)


def normalize(values, gain_row, shift_row):
    middle = jnp.mean(values, axis=-1, keepdims=True)
    centred = values - middle
    spread_sq = jnp.mean(centred * centred, axis=-1, keepdims=True)
    return centred * lax.rsqrt(spread_sq + epsilon) * gain_row + shift_row


def gelu_exact(values):
    return jax.nn.gelu(values, approximate=False)


def fetch_weights(w_qkv, b_qv, w_out, w_up, b_up, w_down, gains, biases):
    gathered = (
        lax.all_gather(w_qkv, "dp", axis=0, tiled=True),
        lax.all_gather(b_qv, "dp", axis=2, tiled=True),
        lax.all_gather(w_out, "dp", axis=1, tiled=True),
        lax.all_gather(w_up, "dp", axis=0, tiled=True),
        lax.all_gather(b_up, "dp", axis=1, tiled=True),
        lax.all_gather(w_down, "dp", axis=1, tiled=True),
    )
    norm_rows = (
        lax.all_gather(gains, ("dp", "mp"), axis=1, tiled=True),
        lax.all_gather(biases, ("dp", "mp"), axis=1, tiled=True),
    )
    return (gathered, norm_rows)


def spread_rows(values):
    return lax.all_gather(values, "mp", axis=0, tiled=True)


def spread_grads(values):
    return lax.all_gather(values, "mp", axis=0, tiled=True)


def project_sum(left, weight, share_rows):

    def term(row_start, row_count):
        row_piece = lax.dynamic_slice_in_dim(left, row_start, row_count, 0)
        return jnp.dot(row_piece, weight, preferred_element_type=jnp.float32)

    return lax.psum_scatter(
        term(jnp.int32(0), share_rows * lax.axis_size("mp")).astype(jnp.bfloat16),
        "mp",
        scatter_dimension=0,
        tiled=True,
    ).astype(jnp.float32)


def project_back(left, weight, share_rows):

    def term(row_start, row_count):
        row_piece = lax.dynamic_slice_in_dim(left, row_start, row_count, 0)
        return lax.dot_general(
            row_piece, weight, (((1,), (1,)), ((), ())), preferred_element_type=jnp.float32
        )

    return lax.psum_scatter(
        term(jnp.int32(0), share_rows * lax.axis_size("mp")).astype(jnp.bfloat16),
        "mp",
        scatter_dimension=0,
        tiled=True,
    ).astype(jnp.float32)


def head_scores(query_head, key_head, same_clip):
    scores = jnp.einsum(
        "qd,kd->qk", query_head, key_head, preferred_element_type=jnp.float32
    ) * HD ** (-0.5)
    return jnp.where(same_clip, scores, masked_score)


def local(frames, clip_ids, w_qkv, b_qv, w_out, w_up, b_up, w_down, gains, biases, cotangent):
    share_rows = frames.shape[1]
    row_total = share_rows * lax.axis_size("mp")
    device = lax.axis_index("dp")
    frame_total = clip_ids.shape[1]
    width_local = w_qkv.shape[2]
    ff_local = w_up.shape[1]
    heads_local = width_local // HD
    reach_devs = (CLIP + row_total - 2) // row_total
    offsets = list(range(-reach_devs, reach_devs + 1))
    window = len(offsets) * row_total
    score_scale = HD ** (-0.5)
    key_place = (device - reach_devs) * row_total + jnp.arange(window, dtype=jnp.int32)
    key_valid = (key_place >= 0) & (key_place < frame_total)
    key_index = jnp.clip(key_place, 0, frame_total - 1)
    query_index = device * row_total + jnp.arange(row_total, dtype=jnp.int32)

    def forward_pass(inputs, clip_row, fetched):
        weights, norm_rows = fetched
        weight_qkv, bias_qv, weight_out, weight_up, bias_up, weight_down = weights
        gain_rows = norm_rows[0].astype(jnp.float32)
        bias_rows = norm_rows[1].astype(jnp.float32)
        key_clip = jnp.where(key_valid, jnp.take(clip_row, key_index), -1)
        query_clip = jnp.take(clip_row, query_index)
        same_clip = query_clip[:, None] == key_clip[None, :]
        resid_in = inputs.astype(jnp.float32)
        normed_one = normalize(resid_in, gain_rows[0], bias_rows[0]).astype(jnp.bfloat16)
        rows_one = spread_rows(normed_one)
        projected = jnp.dot(
            rows_one,
            weight_qkv.reshape(weight_qkv.shape[0], -1),
            preferred_element_type=jnp.float32,
        ).reshape(row_total, 3, width_local)
        bias_pair = bias_qv.reshape(2, width_local).astype(jnp.float32)
        projected = (
            projected + jnp.stack([bias_pair[0], jnp.zeros_like(bias_pair[0]), bias_pair[1]])[None]
        )
        projected = projected.astype(jnp.bfloat16)
        queries = projected[:, 0]
        key_value = projected[:, 1:]
        pieces = []
        for offset in offsets:
            if offset == 0:
                pieces.append(key_value)
            else:
                pieces.append(passed_along(key_value, "dp", -offset))
        near_rows = jnp.concatenate(pieces, axis=0)
        keys_near = near_rows[:, 0]
        values_near = near_rows[:, 1]
        head_outs = []
        log_totals = []
        for head_index in range(heads_local):
            columns = slice(head_index * HD, (head_index + 1) * HD)
            scores = head_scores(queries[:, columns], keys_near[:, columns], same_clip)
            top_score = jnp.max(scores, axis=-1, keepdims=True)
            log_total = top_score + jnp.log(
                jnp.sum(jnp.exp(scores - top_score), axis=-1, keepdims=True)
            )
            soft_weights = jnp.exp(scores - log_total).astype(jnp.bfloat16)
            head_outs.append(
                jnp.dot(soft_weights, values_near[:, columns], preferred_element_type=jnp.float32)
            )
            log_totals.append(log_total)
        attended = jnp.concatenate(head_outs, axis=-1).astype(jnp.bfloat16)
        mixed_rows = resid_in + project_sum(attended, weight_out, share_rows) + bias_rows[1]
        normed_two = normalize(mixed_rows, gain_rows[1], bias_rows[2]).astype(jnp.bfloat16)
        rows_two = spread_rows(normed_two)
        hidden = jnp.dot(rows_two, weight_up, preferred_element_type=jnp.float32) + bias_up.reshape(
            -1
        ).astype(jnp.float32)
        activated = gelu_exact(hidden).astype(jnp.bfloat16)
        result = mixed_rows + project_sum(activated, weight_down, share_rows) + bias_rows[3]
        kept_state = (
            resid_in,
            rows_one,
            queries,
            keys_near,
            values_near,
            same_clip,
            log_totals,
            attended,
            mixed_rows,
            rows_two,
            hidden,
            activated,
            query_clip,
            clip_row,
        )
        return (kept_state, result)

    def backward_pass(kept_state, cot_rows, fetched):
        weights, norm_rows = fetched
        weight_qkv, bias_qv, weight_out, weight_up, bias_up, weight_down = weights
        gain_rows = norm_rows[0].astype(jnp.float32)
        bias_rows = norm_rows[1].astype(jnp.float32)
        (
            resid_in,
            rows_one,
            queries,
            keys_near,
            values_near,
            same_clip,
            log_totals,
            attended,
            mixed_rows,
            rows_two,
            hidden,
            activated,
            query_clip,
            clip_row,
        ) = kept_state
        grad_result = cot_rows.astype(jnp.float32)
        rows_result = spread_grads(grad_result.astype(jnp.bfloat16))
        grad_wdown = jnp.einsum(
            "nf,nd->fd", activated, rows_result, preferred_element_type=jnp.float32
        )
        grad_act = lax.dot_general(
            rows_result, weight_down, (((1,), (1,)), ((), ())), preferred_element_type=jnp.float32
        )
        gelu_pull = jax.vjp(gelu_exact, hidden)[1]
        grad_hidden = gelu_pull(grad_act)[0].astype(jnp.bfloat16)
        grad_wup = jnp.einsum(
            "nd,nf->df", rows_two, grad_hidden, preferred_element_type=jnp.float32
        )
        grad_bup = jnp.sum(grad_hidden, axis=0, dtype=jnp.float32).reshape(1, ff_local)
        grad_two = project_back(grad_hidden, weight_up, share_rows)
        norm_pull_two = jax.vjp(normalize, mixed_rows, gain_rows[1], bias_rows[2])[1]
        grad_mix, grad_gain_two, grad_bias_two = norm_pull_two(grad_two)
        grad_mixed = grad_result + grad_mix
        rows_mixed = spread_grads(grad_mixed.astype(jnp.bfloat16))
        grad_wout = jnp.einsum(
            "nh,nd->hd", attended, rows_mixed, preferred_element_type=jnp.float32
        )
        grad_att = lax.dot_general(
            rows_mixed, weight_out, (((1,), (1,)), ((), ())), preferred_element_type=jnp.float32
        ).astype(jnp.bfloat16)
        query_grads = []
        key_grads = []
        value_grads = []
        row_deltas = []
        for head_index in range(heads_local):
            columns = slice(head_index * HD, (head_index + 1) * HD)
            query_head = queries[:, columns]
            key_head = keys_near[:, columns]
            grad_head = grad_att[:, columns]
            scores = head_scores(query_head, key_head, same_clip)
            soft_weights = jnp.exp(scores - log_totals[head_index])
            grad_soft = jnp.einsum(
                "qd,kd->qk", grad_head, values_near[:, columns], preferred_element_type=jnp.float32
            )
            row_delta = jnp.sum(grad_soft * soft_weights, axis=-1, keepdims=True)
            row_deltas.append(row_delta)
            grad_scores = (soft_weights * (grad_soft - row_delta)).astype(jnp.bfloat16)
            query_grads.append(
                jnp.dot(grad_scores, key_head, preferred_element_type=jnp.float32) * score_scale
            )
            key_grads.append(
                jnp.einsum("qk,qd->kd", grad_scores, query_head, preferred_element_type=jnp.float32)
                * score_scale
            )
            value_grads.append(
                jnp.einsum(
                    "qk,qd->kd",
                    soft_weights.astype(jnp.bfloat16),
                    grad_head,
                    preferred_element_type=jnp.float32,
                )
            )
        grad_queries = jnp.concatenate(query_grads, axis=-1)
        kv_total = jnp.zeros((row_total, 2, width_local), jnp.float32)
        stacked = jnp.stack(
            [jnp.concatenate(key_grads, axis=-1), jnp.concatenate(value_grads, axis=-1)], axis=1
        )
        for place_index, offset in enumerate(offsets):
            segment_grad = stacked[place_index * row_total : (place_index + 1) * row_total]
            if offset == 0:
                kv_total = kv_total + segment_grad
            else:
                kv_total = kv_total + passed_along(shortened(segment_grad), "dp", offset).astype(
                    segment_grad.dtype
                )
        grad_proj = jnp.concatenate([grad_queries[:, None], kv_total], axis=1).astype(jnp.bfloat16)
        grad_wqkv = jnp.einsum(
            "nd,nce->dce", rows_one, grad_proj, preferred_element_type=jnp.float32
        )
        grad_bqv = jnp.stack(
            [
                jnp.sum(grad_proj[:, 0], axis=0, dtype=jnp.float32),
                jnp.sum(grad_proj[:, 2], axis=0, dtype=jnp.float32),
            ]
        ).reshape(2, 1, width_local)
        grad_one = project_back(
            grad_proj.reshape(row_total, -1),
            weight_qkv.reshape(weight_qkv.shape[0], -1),
            share_rows,
        )
        norm_pull_one = jax.vjp(normalize, resid_in, gain_rows[0], bias_rows[0])[1]
        grad_in_norm, grad_gain_one, grad_bias_one = norm_pull_one(grad_one)
        grad_inputs = (grad_mixed + grad_in_norm).astype(jnp.bfloat16)
        grad_gain_rows = jnp.stack([grad_gain_one, grad_gain_two])
        grad_bias_rows = jnp.stack(
            [
                grad_bias_one,
                jnp.sum(grad_mixed, axis=0),
                grad_bias_two,
                jnp.sum(grad_result, axis=0),
            ]
        )
        grad_parts = (
            grad_wqkv,
            grad_bqv,
            grad_wout,
            grad_wup,
            grad_bup,
            grad_wdown,
            grad_gain_rows,
            grad_bias_rows,
        )
        return (grad_parts, grad_inputs)

    def step(totals, step_items):
        inputs, clip_row, cot_rows = step_items
        front_weights = fetch_weights(w_qkv, b_qv, w_out, w_up, b_up, w_down, gains, biases)
        kept_state, result = forward_pass(inputs, clip_row, front_weights)
        fenced = lax.optimization_barrier(
            (w_qkv, b_qv, w_out, w_up, b_up, w_down, gains, biases, result)
        )
        behind = fetch_weights(
            fenced[0], fenced[1], fenced[2], fenced[3], fenced[4], fenced[5], fenced[6], fenced[7]
        )
        grad_parts, grad_inputs = backward_pass(kept_state, cot_rows, behind)
        totals = tuple((running + grad_part for running, grad_part in zip(totals, grad_parts)))
        return (totals, (result.astype(jnp.bfloat16), grad_inputs))

    zeros_start = (
        jnp.zeros((D, 3, width_local), jnp.float32),
        jnp.zeros((2, 1, width_local), jnp.float32),
        jnp.zeros((width_local, D), jnp.float32),
        jnp.zeros((D, ff_local), jnp.float32),
        jnp.zeros((1, ff_local), jnp.float32),
        jnp.zeros((ff_local, D), jnp.float32),
        jnp.zeros((2, D), jnp.float32),
        jnp.zeros((4, D), jnp.float32),
    )
    totals, (output, frames_grad) = lax.scan(step, zeros_start, (frames, clip_ids, cotangent))
    owned = (
        lax.psum_scatter(totals[0], "dp", scatter_dimension=0, tiled=True),
        lax.psum_scatter(totals[1], "dp", scatter_dimension=2, tiled=True),
        lax.psum_scatter(totals[2], "dp", scatter_dimension=1, tiled=True),
        lax.psum_scatter(totals[3], "dp", scatter_dimension=0, tiled=True),
        lax.psum_scatter(totals[4], "dp", scatter_dimension=1, tiled=True),
        lax.psum_scatter(totals[5], "dp", scatter_dimension=1, tiled=True),
    )
    owned_norms = (
        lax.psum_scatter(totals[6], ("dp", "mp"), scatter_dimension=1, tiled=True),
        lax.psum_scatter(totals[7], ("dp", "mp"), scatter_dimension=1, tiled=True),
    )
    return (
        output,
        frames_grad,
        owned[0],
        owned[1],
        owned[2],
        owned[3],
        owned[4],
        owned[5],
        owned_norms[0],
        owned_norms[1],
    )


def solution(mesh):
    placed = (
        P(None, ("dp", "mp"), None),
        P(),
        P("dp", None, "mp"),
        P(None, "mp", "dp"),
        P("mp", "dp"),
        P("dp", "mp"),
        P("mp", "dp"),
        P("mp", "dp"),
        P(None, ("dp", "mp")),
        P(None, ("dp", "mp")),
        P(None, ("dp", "mp"), None),
    )
    return jax.shard_map(
        local,
        mesh=mesh,
        in_specs=placed,
        out_specs=(
            P(None, ("dp", "mp"), None),
            P(None, ("dp", "mp"), None),
            P("dp", None, "mp"),
            P(None, "mp", "dp"),
            P("mp", "dp"),
            P("dp", "mp"),
            P("mp", "dp"),
            P("mp", "dp"),
            P(None, ("dp", "mp")),
            P(None, ("dp", "mp")),
        ),
        check_vma=False,
    )
```

profile of v0, /device:TPU:0, one launch (start us, length us, event | category | flops | bytes accessed | tf_op | source)
XLA Modules:
  0.0 3567.6 jit_solution(23908522268389208)
XLA Ops:
  9.8 3199.7 %while.31 = (s32[]{:T(128)}, f32[768,3,192]{0,2,1:T(8,128)}, f32[2,1,192]{2,1,0:T(1,128)}, f32[192,768]{1,0:T(8,128)}, f32[768,768]{1,0:T(8,128)}, /*index=5*/f3...) while((s32[]{:T(128)}, f32[768,3,192]{0,2,1:T(8,128)}, ...), condition=%wide.region_31.32_spmd.clone.clone.clone, body=%wide.region_0.31_spmd.clone.clone.clone.sunk | while | flops 11638805504 | bytes 781726784 | solution.py:341
  12.6 43.5 %all-gather.21 = bf16[32,24,2]{1,2,0:T(2,128)(2,1)S(1)} all-gather(bf16[1,24,2]{1,2,0:T(2,128)(2,1)} %bitcast.337), channel_id=1, replica_groups=mesh['dp'=8,'mp'=4] {'dp','mp'}, dimensions={0}, use_global_device_ids=true | all-gather | bytes 3168 | tf_op jit(solution)/shard_map/while/body/eval_jaxpr/all_gather | solution.py:46
  56.3 37.0 %all-gather.20 = bf16[32,24,4]{1,2,0:T(4,128)(2,1)S(1)} all-gather(bf16[1,24,4]{1,2,0:T(4,128)(2,1)} %bitcast.340), channel_id=1, replica_groups=mesh['dp'=8,'mp'=4] {'dp','mp'}, dimensions={0}, use_global_device_ids=true | all-gather | bytes 6336 | tf_op jit(solution)/shard_map/while/body/eval_jaxpr/all_gather | solution.py:47
  136.8 37.0 %all_gather.99 = bf16[768,3,192]{2,1,0:T(4,128)(2,1)S(1)} all-gather(bf16[96,3,192]{2,1,0:T(4,128)(2,1)S(1)} %copy.86), channel_id=1, replica_groups=mesh['dp'=8,'mp'=4] {'dp'}, dimensions={0}, use_global_device_ids=true | all-gather | bytes 995328 | tf_op jit(solution)/shard_map/while/body/eval_jaxpr/all_gather | solution.py:38
  521.0 38.9 %all-gather.23 = bf16[32,24,2]{1,2,0:T(2,128)(2,1)S(1)} all-gather(bf16[1,24,2]{1,2,0:T(2,128)(2,1)S(1)} %bitcast.338), channel_id=1, replica_groups=mesh['dp'=8,'mp'=4] {'dp','mp'}, dimensions={0}, use_global_device_ids=true | all-gather | bytes 3168 | tf_op jit(solution)/shard_map/while/body/eval_jaxpr/all_gather | solution.py:46
  593.8 37.0 %all_gather.110 = bf16[768,3,192]{2,0,1:T(8,128)(2,1)} all-gather(bf16[96,3,192]{2,0,1:T(8,128)(2,1)S(1)} %copy-done.32), channel_id=1, replica_groups=mesh['dp'=8,'mp'=4] {'dp'}, dimensions={0}, use_global_device_ids=true | all-gather | bytes 995328 | tf_op jit(solution)/shard_map/while/body/eval_jaxpr/all_gather | solution.py:38
  811.7 40.7 %all-gather.21 = bf16[32,24,2]{1,2,0:T(2,128)(2,1)S(1)} all-gather(bf16[1,24,2]{1,2,0:T(2,128)(2,1)} %bitcast.337), channel_id=1, replica_groups=mesh['dp'=8,'mp'=4] {'dp','mp'}, dimensions={0}, use_global_device_ids=true | all-gather | bytes 3168 | tf_op jit(solution)/shard_map/while/body/eval_jaxpr/all_gather | solution.py:46
  852.8 37.0 %all-gather.20 = bf16[32,24,4]{1,2,0:T(4,128)(2,1)S(1)} all-gather(bf16[1,24,4]{1,2,0:T(4,128)(2,1)} %bitcast.340), channel_id=1, replica_groups=mesh['dp'=8,'mp'=4] {'dp','mp'}, dimensions={0}, use_global_device_ids=true | all-gather | bytes 6336 | tf_op jit(solution)/shard_map/while/body/eval_jaxpr/all_gather | solution.py:47
  933.3 37.0 %all_gather.99 = bf16[768,3,192]{2,1,0:T(4,128)(2,1)S(1)} all-gather(bf16[96,3,192]{2,1,0:T(4,128)(2,1)S(1)} %copy.86), channel_id=1, replica_groups=mesh['dp'=8,'mp'=4] {'dp'}, dimensions={0}, use_global_device_ids=true | all-gather | bytes 995328 | tf_op jit(solution)/shard_map/while/body/eval_jaxpr/all_gather | solution.py:38
  1318.7 38.9 %all-gather.23 = bf16[32,24,2]{1,2,0:T(2,128)(2,1)S(1)} all-gather(bf16[1,24,2]{1,2,0:T(2,128)(2,1)S(1)} %bitcast.338), channel_id=1, replica_groups=mesh['dp'=8,'mp'=4] {'dp','mp'}, dimensions={0}, use_global_device_ids=true | all-gather | bytes 3168 | tf_op jit(solution)/shard_map/while/body/eval_jaxpr/all_gather | solution.py:46
  1391.5 37.0 %all_gather.110 = bf16[768,3,192]{2,0,1:T(8,128)(2,1)} all-gather(bf16[96,3,192]{2,0,1:T(8,128)(2,1)S(1)} %copy-done.32), channel_id=1, replica_groups=mesh['dp'=8,'mp'=4] {'dp'}, dimensions={0}, use_global_device_ids=true | all-gather | bytes 995328 | tf_op jit(solution)/shard_map/while/body/eval_jaxpr/all_gather | solution.py:38
  1611.1 40.7 %all-gather.21 = bf16[32,24,2]{1,2,0:T(2,128)(2,1)S(1)} all-gather(bf16[1,24,2]{1,2,0:T(2,128)(2,1)} %bitcast.337), channel_id=1, replica_groups=mesh['dp'=8,'mp'=4] {'dp','mp'}, dimensions={0}, use_global_device_ids=true | all-gather | bytes 3168 | tf_op jit(solution)/shard_map/while/body/eval_jaxpr/all_gather | solution.py:46
  1652.1 37.0 %all-gather.20 = bf16[32,24,4]{1,2,0:T(4,128)(2,1)S(1)} all-gather(bf16[1,24,4]{1,2,0:T(4,128)(2,1)} %bitcast.340), channel_id=1, replica_groups=mesh['dp'=8,'mp'=4] {'dp','mp'}, dimensions={0}, use_global_device_ids=true | all-gather | bytes 6336 | tf_op jit(solution)/shard_map/while/body/eval_jaxpr/all_gather | solution.py:47
  1732.6 37.0 %all_gather.99 = bf16[768,3,192]{2,1,0:T(4,128)(2,1)S(1)} all-gather(bf16[96,3,192]{2,1,0:T(4,128)(2,1)S(1)} %copy.86), channel_id=1, replica_groups=mesh['dp'=8,'mp'=4] {'dp'}, dimensions={0}, use_global_device_ids=true | all-gather | bytes 995328 | tf_op jit(solution)/shard_map/while/body/eval_jaxpr/all_gather | solution.py:38
  2117.9 38.9 %all-gather.23 = bf16[32,24,2]{1,2,0:T(2,128)(2,1)S(1)} all-gather(bf16[1,24,2]{1,2,0:T(2,128)(2,1)S(1)} %bitcast.338), channel_id=1, replica_groups=mesh['dp'=8,'mp'=4] {'dp','mp'}, dimensions={0}, use_global_device_ids=true | all-gather | bytes 3168 | tf_op jit(solution)/shard_map/while/body/eval_jaxpr/all_gather | solution.py:46
  2410.3 40.7 %all-gather.21 = bf16[32,24,2]{1,2,0:T(2,128)(2,1)S(1)} all-gather(bf16[1,24,2]{1,2,0:T(2,128)(2,1)} %bitcast.337), channel_id=1, replica_groups=mesh['dp'=8,'mp'=4] {'dp','mp'}, dimensions={0}, use_global_device_ids=true | all-gather | bytes 3168 | tf_op jit(solution)/shard_map/while/body/eval_jaxpr/all_gather | solution.py:46
  2451.4 37.0 %all-gather.20 = bf16[32,24,4]{1,2,0:T(4,128)(2,1)S(1)} all-gather(bf16[1,24,4]{1,2,0:T(4,128)(2,1)} %bitcast.340), channel_id=1, replica_groups=mesh['dp'=8,'mp'=4] {'dp','mp'}, dimensions={0}, use_global_device_ids=true | all-gather | bytes 6336 | tf_op jit(solution)/shard_map/while/body/eval_jaxpr/all_gather | solution.py:47
  2531.9 37.0 %all_gather.99 = bf16[768,3,192]{2,1,0:T(4,128)(2,1)S(1)} all-gather(bf16[96,3,192]{2,1,0:T(4,128)(2,1)S(1)} %copy.86), channel_id=1, replica_groups=mesh['dp'=8,'mp'=4] {'dp'}, dimensions={0}, use_global_device_ids=true | all-gather | bytes 995328 | tf_op jit(solution)/shard_map/while/body/eval_jaxpr/all_gather | solution.py:38
  2917.1 38.9 %all-gather.23 = bf16[32,24,2]{1,2,0:T(2,128)(2,1)S(1)} all-gather(bf16[1,24,2]{1,2,0:T(2,128)(2,1)S(1)} %bitcast.338), channel_id=1, replica_groups=mesh['dp'=8,'mp'=4] {'dp','mp'}, dimensions={0}, use_global_device_ids=true | all-gather | bytes 3168 | tf_op jit(solution)/shard_map/while/body/eval_jaxpr/all_gather | solution.py:46
  3243.4 37.3 %all-reduce.7 = (f32[2,768]{1,0:T(2,128)S(1)}, f32[4,768]{1,0:T(4,128)S(1)}) all-reduce(f32[2,768]{1,0:T(2,128)S(1)} %copy-done.55, f32[4,768]{1,0:T(4,128)S(1)} %copy-done.42), channel_id=13, replica_groups=mesh['dp'=8,'mp'=4] {'dp','mp'}, use_global_device_ids=true, to_apply=%region_38.39.clone | all-reduce | flops 4608 | bytes 36864
  3284.1 56.9 %reduce-scatter.23.cloned.1.call-done = f32[96,192]{1,0:T(8,128)} async-done(((f32[768,192]{1,0:T(8,128)}), f32[96,192]{1,0:T(8,128)}) %reduce-scatter.23.cloned.1.call-update) | async-done | bytes 73744
  3342.6 71.2 %reduce-scatter.17.cloned.1.call-done = f32[96,3,192]{2,0,1:T(8,128)} async-done(((f32[768,3,192]{2,0,1:T(8,128)}), f32[96,3,192]{2,0,1:T(8,128)}) %reduce-scatter.17.cloned.1.call-update) | async-done | bytes 221200 | tf_op jit(solution)/shard_map/reduce_scatter | solution.py:343
  3413.8 72.8 %reduce-scatter.19.cloned.1.call-done = f32[96,768]{1,0:T(8,128)} async-done(((f32[768,768]{1,0:T(8,128)}), f32[96,768]{1,0:T(8,128)}) %reduce-scatter.19.cloned.1.call-update) | async-done | bytes 294928 | tf_op jit(solution)/shard_map/reduce_scatter | solution.py:346
  3486.6 73.1 %reduce-scatter.21.cloned.1.call-done = f32[768,96]{0,1:T(8,128)} async-done(((f32[768,768]{0,1:T(8,128)}), f32[768,96]{0,1:T(8,128)}) %reduce-scatter.21.cloned.1.call-update) | async-done | bytes 294928 | tf_op jit(solution)/shard_map/reduce_scatter | solution.py:348
  (1402 shorter events, 2535.5 us)
Async XLA Ops:
  10.3 330.0 %reduce-scatter.27.cloned.1.call-start = ((), (), s32[]{:S(2)}) async-start(), calls=%async_computation.14 | async-start | bytes 1105920 | tf_op jit(solution)/shard_map/while/body/eval_jaxpr/reduce_scatter | solution.py:66
  311.6 90.4 %all-gather.31.cloned.1.call-start = ((), (), s32[]{:S(2)}) async-start(), calls=%async_computation.16 | async-start | bytes 1327104 | tf_op jit(solution)/shard_map/while/body/eval_jaxpr/all_gather | solution.py:43
  312.2 115.5 %reduce-scatter.29.cloned.1.call-start = ((), (), s32[]{:S(2)}) async-start(), calls=%async_computation.17 | async-start | bytes 1105920 | tf_op jit(solution)/shard_map/while/body/eval_jaxpr/reduce_scatter | solution.py:66
  430.2 203.2 %reduce-scatter.31.cloned.1.call-start = ((), (), s32[]{:S(2)}) async-start(), calls=%async_computation.20 | async-start | bytes 1105920 | tf_op jit(solution)/shard_map/while/body/eval_jaxpr/reduce_scatter | solution.py:82
  516.4 288.1 %reduce-scatter.33.cloned.1.call-start = ((), (), s32[]{:S(2)}) async-start(), calls=%async_computation.21 | async-start | bytes 1105920 | tf_op jit(solution)/shard_map/while/body/eval_jaxpr/reduce_scatter | solution.py:82
  809.4 327.2 %reduce-scatter.27.cloned.1.call-start = ((), (), s32[]{:S(2)}) async-start(), calls=%async_computation.14 | async-start | bytes 1105920 | tf_op jit(solution)/shard_map/while/body/eval_jaxpr/reduce_scatter | solution.py:66
  1108.2 90.8 %all-gather.31.cloned.1.call-start = ((), (), s32[]{:S(2)}) async-start(), calls=%async_computation.16 | async-start | bytes 1327104 | tf_op jit(solution)/shard_map/while/body/eval_jaxpr/all_gather | solution.py:43
  1108.9 115.8 %reduce-scatter.29.cloned.1.call-start = ((), (), s32[]{:S(2)}) async-start(), calls=%async_computation.17 | async-start | bytes 1105920 | tf_op jit(solution)/shard_map/while/body/eval_jaxpr/reduce_scatter | solution.py:66
  1227.1 205.7 %reduce-scatter.31.cloned.1.call-start = ((), (), s32[]{:S(2)}) async-start(), calls=%async_computation.20 | async-start | bytes 1105920 | tf_op jit(solution)/shard_map/while/body/eval_jaxpr/reduce_scatter | solution.py:82
  1313.2 290.6 %reduce-scatter.33.cloned.1.call-start = ((), (), s32[]{:S(2)}) async-start(), calls=%async_computation.21 | async-start | bytes 1105920 | tf_op jit(solution)/shard_map/while/body/eval_jaxpr/reduce_scatter | solution.py:82
  1608.8 327.2 %reduce-scatter.27.cloned.1.call-start = ((), (), s32[]{:S(2)}) async-start(), calls=%async_computation.14 | async-start | bytes 1105920 | tf_op jit(solution)/shard_map/while/body/eval_jaxpr/reduce_scatter | solution.py:66
  1907.4 90.7 %all-gather.31.cloned.1.call-start = ((), (), s32[]{:S(2)}) async-start(), calls=%async_computation.16 | async-start | bytes 1327104 | tf_op jit(solution)/shard_map/while/body/eval_jaxpr/all_gather | solution.py:43
  1908.1 115.7 %reduce-scatter.29.cloned.1.call-start = ((), (), s32[]{:S(2)}) async-start(), calls=%async_computation.17 | async-start | bytes 1105920 | tf_op jit(solution)/shard_map/while/body/eval_jaxpr/reduce_scatter | solution.py:66
  2026.3 205.7 %reduce-scatter.31.cloned.1.call-start = ((), (), s32[]{:S(2)}) async-start(), calls=%async_computation.20 | async-start | bytes 1105920 | tf_op jit(solution)/shard_map/while/body/eval_jaxpr/reduce_scatter | solution.py:82
  2112.5 290.6 %reduce-scatter.33.cloned.1.call-start = ((), (), s32[]{:S(2)}) async-start(), calls=%async_computation.21 | async-start | bytes 1105920 | tf_op jit(solution)/shard_map/while/body/eval_jaxpr/reduce_scatter | solution.py:82
  2408.0 327.2 %reduce-scatter.27.cloned.1.call-start = ((), (), s32[]{:S(2)}) async-start(), calls=%async_computation.14 | async-start | bytes 1105920 | tf_op jit(solution)/shard_map/while/body/eval_jaxpr/reduce_scatter | solution.py:66
  2706.6 90.6 %all-gather.31.cloned.1.call-start = ((), (), s32[]{:S(2)}) async-start(), calls=%async_computation.16 | async-start | bytes 1327104 | tf_op jit(solution)/shard_map/while/body/eval_jaxpr/all_gather | solution.py:43
  2707.4 115.6 %reduce-scatter.29.cloned.1.call-start = ((), (), s32[]{:S(2)}) async-start(), calls=%async_computation.17 | async-start | bytes 1105920 | tf_op jit(solution)/shard_map/while/body/eval_jaxpr/reduce_scatter | solution.py:66
  2825.5 205.7 %reduce-scatter.31.cloned.1.call-start = ((), (), s32[]{:S(2)}) async-start(), calls=%async_computation.20 | async-start | bytes 1105920 | tf_op jit(solution)/shard_map/while/body/eval_jaxpr/reduce_scatter | solution.py:82
  2911.7 290.6 %reduce-scatter.33.cloned.1.call-start = ((), (), s32[]{:S(2)}) async-start(), calls=%async_computation.21 | async-start | bytes 1105920 | tf_op jit(solution)/shard_map/while/body/eval_jaxpr/reduce_scatter | solution.py:82
  3211.2 129.8 %reduce-scatter.23.cloned.1.call-start = ((), (), s32[]{:S(2)}) async-start(), calls=%async_computation.12 | async-start | bytes 884736
  3213.5 200.3 %reduce-scatter.17.cloned.1.call-start = ((), (), s32[]{:S(2)}) async-start(), calls=%async_computation.9 | async-start | bytes 2654208 | tf_op jit(solution)/shard_map/reduce_scatter | solution.py:343
  3216.5 270.0 %reduce-scatter.19.cloned.1.call-start = ((), (), s32[]{:S(2)}) async-start(), calls=%async_computation.10 | async-start | bytes 2654208 | tf_op jit(solution)/shard_map/reduce_scatter | solution.py:346
  3217.1 342.6 %reduce-scatter.21.cloned.1.call-start = ((), (), s32[]{:S(2)}) async-start(), calls=%async_computation.11 | async-start | bytes 2654208 | tf_op jit(solution)/shard_map/reduce_scatter | solution.py:348
  (374 other events, 10463.3 us)
Sparse Core Ops, SparseCore 0:
  311.1 29.0 reduce-scatter.26
  405.5 22.1 reduce-scatter.28
  516.5 22.1 reduce-scatter.30
  763.3 41.1 reduce-scatter.32
  1107.5 29.0 reduce-scatter.26
  1202.5 22.1 reduce-scatter.28
  1313.4 22.1 reduce-scatter.30
  1562.6 41.1 reduce-scatter.32
  1906.9 29.0 reduce-scatter.26
  2001.6 22.1 reduce-scatter.28
  2112.6 22.1 reduce-scatter.30
  2361.9 41.1 reduce-scatter.32
  2706.2 29.0 reduce-scatter.26
  2800.8 22.1 reduce-scatter.28
  2911.8 22.1 reduce-scatter.30
  3161.1 41.1 reduce-scatter.32
  3213.2 62.2 reduce-scatter.24
  3278.7 62.2 reduce-scatter.22
  3345.0 68.7 reduce-scatter.16
  3417.7 68.8 reduce-scatter.18
  3490.6 68.9 reduce-scatter.20
Sparse Core Ops, SparseCore 1:
  313.7 46.4 all-gather.28
  362.2 39.7 all-gather.30
  429.5 41.4 all-gather.32
  473.2 39.7 all-gather.34
  1110.4 46.4 all-gather.28
  1159.1 39.9 all-gather.30
  1226.5 41.4 all-gather.32
  1270.1 39.7 all-gather.34
  1909.4 46.5 all-gather.28
  1958.3 39.7 all-gather.30
  2025.6 41.4 all-gather.32
  2069.3 39.7 all-gather.34
  2708.7 46.5 all-gather.28
  2757.5 39.7 all-gather.30
  2824.8 41.4 all-gather.32
  2868.5 39.7 all-gather.34
where the time goes:
time: 3580 us; the launch traced here: 3570 us
  blocking collectives  1450 us (41%)
  waiting for transfers between devices  1050 us (29%)
  matrix products  374 us (10%)
  other arithmetic  347 us (10%)
  local copies, waits for them, and re-layouts  192 us (5%)
  starting transfers between devices  122 us (3%)
    all_gather x8, blocking collectives, fetch_weights(): lax.all_gather(gains, ('dp', 'mp'), axis=1, tiled=True)  321 us
    all_gather x8, blocking collectives, fetch_weights(): lax.all_gather(w_qkv, 'dp', axis=0, tiled=True)  296 us
    all_gather x8, blocking collectives, fetch_weights(): lax.all_gather(w_out, 'dp', axis=1, tiled=True)  267 us
    all_gather x8, waiting for transfers between devices, fetch_weights(): lax.all_gather(w_down, 'dp', axis=1, tiled=True)  260 us
    all_gather x8, waiting for transfers between devices, fetch_weights(): lax.all_gather(w_up, 'dp', axis=0, tiled=True)  175 us
    all_gather x4, blocking collectives, fetch_weights(): lax.all_gather(biases, ('dp', 'mp'), axis=1, tiled=True)  148 us
    convert_element_type x12, other arithmetic, backward_pass(): grad_scores = (soft_weights * (grad_soft - row_delta)).astype(jnp.bfloat16)  139 us
    reduce_scatter x8, waiting for transfers between devices, project_back(): lax.psum_scatter(term(jnp.int32(0), share_rows * lax.axis_size('mp')).ast...  135 us
  transfers between devices with their start and end apart: 85, of which 52 were waited for; matrix products, arithmetic and copies ran while one was open for 8% of the time, Pallas kernels for 0%

commit v1 on v0

v1 whole, which is shorter than its diff:
```python
import functools

import jax
import jax.numpy as jnp
from jax import lax
from jax.experimental import pallas as pl
from jax.experimental.pallas import tpu as pltpu
from jax.sharding import Mesh, PartitionSpec as P

HD = 64
EPS = 1e-05
MASKED = -1e30
SCALE = HD ** (-0.5)
ALL = ("mb", "part", "mp")
OWNER = ("mp", "mb", "part")
PLANE = ("part", "mp")
bf16 = jnp.bfloat16
f32 = jnp.float32
QT = 288
KT = 256

NT = (((1,), (1,)), ((), ()))
TN = (((0,), (0,)), ((), ()))


def dot(a, b, dims=(((1,), (0,)), ((), ()))):
    return lax.dot_general(a, b, dims, preferred_element_type=f32)


def tile_span(span_ref, tile, base, block):
    first = jnp.maximum(span_ref[0, tile] - base, 0) // KT
    last = (jnp.minimum(span_ref[1, tile] - base, block) + (KT - 1)) // KT
    return first, jnp.maximum(last, first)


def attend_kernel(span_ref, q_ref, qid_ref, kid_ref, kv_ref, att_ref, lse_ref, m_ref, l_ref, acc_ref, *, heads, block):
    step = pl.program_id(0)
    steps = pl.num_programs(0)
    tiles = q_ref.shape[0] // QT

    @pl.when(step == 0)
    def _():
        m_ref[...] = jnp.full(m_ref.shape, MASKED, f32)
        l_ref[...] = jnp.zeros(l_ref.shape, f32)
        acc_ref[...] = jnp.zeros(acc_ref.shape, f32)

    def one_tile(tile, _):
        rows = pl.ds(pl.multiple_of(tile * QT, QT), QT)
        q_all = q_ref[rows, :]
        qid = qid_ref[rows, :]
        queries = [
            jnp.concatenate(
                [q_all[:, h * HD : (h + 1) * HD] * bf16(SCALE), jnp.zeros((QT, HD), bf16)], axis=1
            )
            for h in range(heads)
        ]
        first, last = tile_span(span_ref, tile, step * block, block)

        def body(kt, state):
            cols = pl.ds(pl.multiple_of(kt * KT, KT), KT)
            same = qid == kid_ref[0, :, cols]
            out = []
            for h in range(heads):
                m, l, acc = state[h]
                kv = kv_ref[cols, h * 128 : (h + 1) * 128]
                s = jnp.where(same, dot(queries[h], kv, NT), MASKED)
                m_new = jnp.maximum(m, jnp.max(s, axis=1, keepdims=True))
                p = jnp.exp(s - m_new)
                keep = jnp.exp(m - m_new)
                out.append(
                    (
                        m_new,
                        l * keep + jnp.sum(p, axis=1, keepdims=True),
                        acc * keep + dot(p.astype(bf16), kv),
                    )
                )
            return tuple(out)

        state = tuple(
            (m_ref[h, rows, :], l_ref[h, rows, :], acc_ref[h, rows, :]) for h in range(heads)
        )
        state = lax.fori_loop(first, last, body, state)
        for h in range(heads):
            m_ref[h, rows, :] = state[h][0]
            l_ref[h, rows, :] = state[h][1]
            acc_ref[h, rows, :] = state[h][2]

        @pl.when(step == steps - 1)
        def _():
            outs = []
            for h in range(heads):
                m, l, acc = state[h]
                outs.append((acc / l)[:, HD:])
                lse_ref[h, rows, :] = m + jnp.log(l)
            att_ref[rows, :] = jnp.concatenate(outs, axis=1).astype(bf16)

        return 0

    lax.fori_loop(0, tiles, one_tile, 0)


def attend(span, q, qid, kid, kv, heads, block):
    rows = q.shape[0]
    whole = lambda s, _: (0, 0)
    return pl.pallas_call(
        functools.partial(attend_kernel, heads=heads, block=block),
        grid_spec=pltpu.PrefetchScalarGridSpec(
            num_scalar_prefetch=1,
            grid=(kv.shape[0] // block,),
            in_specs=[
                pl.BlockSpec(q.shape, whole),
                pl.BlockSpec(qid.shape, whole),
                pl.BlockSpec((1, 1, block), lambda s, _: (s, 0, 0)),
                pl.BlockSpec((block, kv.shape[1]), lambda s, _: (s, 0)),
            ],
            out_specs=[
                pl.BlockSpec(q.shape, whole),
                pl.BlockSpec((heads, rows, 1), lambda s, _: (0, 0, 0)),
            ],
            scratch_shapes=[
                pltpu.VMEM((heads, rows, 1), f32),
                pltpu.VMEM((heads, rows, 1), f32),
                pltpu.VMEM((heads, rows, 128), f32),
            ],
        ),
        out_shape=[
            jax.ShapeDtypeStruct(q.shape, bf16),
            jax.ShapeDtypeStruct((heads, rows, 1), f32),
        ],
        name="attend",
    )(span, q, qid, kid, kv)


def pull_kernel(span_ref, q_ref, qid_ref, kid_ref, kv_ref, datt_ref, att_ref, lse_ref, dq_ref, dkv_ref, dq_acc, dkv_acc, *, heads, block):
    step = pl.program_id(0)
    steps = pl.num_programs(0)
    tiles = q_ref.shape[0] // QT

    @pl.when(step == 0)
    def _():
        dq_acc[...] = jnp.zeros(dq_acc.shape, f32)

    dkv_acc[...] = jnp.zeros(dkv_acc.shape, f32)

    def one_tile(tile, _):
        rows = pl.ds(pl.multiple_of(tile * QT, QT), QT)
        q_all = q_ref[rows, :]
        d_all = datt_ref[rows, :]
        qid = qid_ref[rows, :]
        both = d_all.astype(f32) * att_ref[rows, :].astype(f32)
        blank = jnp.zeros((QT, HD), bf16)
        queries, pulls, deltas, lses = [], [], [], []
        for h in range(heads):
            cut = slice(h * HD, (h + 1) * HD)
            queries.append(jnp.concatenate([q_all[:, cut] * bf16(SCALE), blank], axis=1))
            pulls.append(jnp.concatenate([blank, d_all[:, cut]], axis=1))
            deltas.append(jnp.sum(both[:, cut], axis=1, keepdims=True))
            lses.append(lse_ref[h, rows, :])
        stacks = [jnp.concatenate([queries[h], pulls[h]], axis=0) for h in range(heads)]
        first, last = tile_span(span_ref, tile, step * block, block)

        def body(kt, state):
            cols = pl.ds(pl.multiple_of(kt * KT, KT), KT)
            same = qid == kid_ref[0, :, cols]
            out = []
            for h in range(heads):
                kv = kv_ref[cols, h * 128 : (h + 1) * 128]
                s = jnp.where(same, dot(queries[h], kv, NT), MASKED)
                p = jnp.exp(s - lses[h])
                dp = dot(pulls[h], kv, NT)
                ds = (p * (dp - deltas[h])).astype(bf16)
                out.append(state[h] + dot(ds, kv))
                pair = jnp.concatenate([ds, p.astype(bf16)], axis=0)
                dkv_acc[cols, h * 128 : (h + 1) * 128] += dot(pair, stacks[h], TN)
            return tuple(out)

        state = tuple(dq_acc[h, rows, :] for h in range(heads))
        state = lax.fori_loop(first, last, body, state)
        for h in range(heads):
            dq_acc[h, rows, :] = state[h]

        @pl.when(step == steps - 1)
        def _():
            dq_ref[rows, :] = jnp.concatenate(
                [state[h][:, :HD] * SCALE for h in range(heads)], axis=1
            ).astype(bf16)

        return 0

    lax.fori_loop(0, tiles, one_tile, 0)
    dkv_ref[...] = dkv_acc[...].astype(bf16)


def attend_pull(span, q, qid, kid, kv, datt, att, lse, heads, block):
    rows = q.shape[0]
    whole = lambda s, _: (0, 0)
    return pl.pallas_call(
        functools.partial(pull_kernel, heads=heads, block=block),
        grid_spec=pltpu.PrefetchScalarGridSpec(
            num_scalar_prefetch=1,
            grid=(kv.shape[0] // block,),
            in_specs=[
                pl.BlockSpec(q.shape, whole),
                pl.BlockSpec(qid.shape, whole),
                pl.BlockSpec((1, 1, block), lambda s, _: (s, 0, 0)),
                pl.BlockSpec((block, kv.shape[1]), lambda s, _: (s, 0)),
                pl.BlockSpec(q.shape, whole),
                pl.BlockSpec(q.shape, whole),
                pl.BlockSpec((heads, rows, 1), lambda s, _: (0, 0, 0)),
            ],
            out_specs=[
                pl.BlockSpec(q.shape, whole),
                pl.BlockSpec((block, kv.shape[1]), lambda s, _: (s, 0)),
            ],
            scratch_shapes=[
                pltpu.VMEM((heads, rows, 128), f32),
                pltpu.VMEM((block, kv.shape[1]), f32),
            ],
        ),
        out_shape=[
            jax.ShapeDtypeStruct(q.shape, bf16),
            jax.ShapeDtypeStruct(kv.shape, bf16),
        ],
        name="attend_pull",
    )(span, q, qid, kid, kv, datt, att, lse)


def standard(values):
    middle = jnp.mean(values, axis=-1, keepdims=True)
    centred = values - middle
    inverse = lax.rsqrt(jnp.mean(centred * centred, axis=-1, keepdims=True) + EPS)
    return centred * inverse, inverse


def norm_pull(grad, hat, inverse, gain):
    t = grad * gain
    return (t - jnp.mean(t, axis=-1, keepdims=True) - hat * jnp.mean(t * hat, axis=-1, keepdims=True)) * inverse


def gelu_exact(values):
    return jax.nn.gelu(values, approximate=False)


def local(frames, clip_ids, w_qkv, b_qv, w_out, w_up, b_up, w_down, gains, biases, cotangent):
    mbs, share, width = frames.shape
    mp = lax.axis_size("mp")
    parts = lax.axis_size("part")
    dp = parts * mbs
    rows = mbs * share
    seq = rows * parts * mp
    head_cols = w_qkv.shape[2]
    heads = head_cols // HD
    ff = w_up.shape[1]
    band = w_qkv.shape[0]
    piece = rows // parts
    half = piece // 2
    my_part = lax.axis_index("part")
    my_mp = lax.axis_index("mp")
    flip = (my_mp // 2) % 2 == 1

    kv_shard = jnp.stack(
        [w_qkv[:, 1].reshape(band, heads, HD), w_qkv[:, 2].reshape(band, heads, HD)], axis=2
    ).reshape(band, 2 * head_cols)
    qkv_shard = jnp.concatenate([w_qkv[:, 0], kv_shard], axis=1)
    smalls = (b_qv, b_up, gains, biases)
    small_sizes = [s.size for s in smalls]
    line = jnp.concatenate([s.reshape(-1) for s in smalls])
    wide = 3 * head_cols
    tall = (band + 1 + 15) // 16 * 16
    line = jnp.pad(line, (0, wide - line.shape[0]))[None]
    shard_one = jnp.concatenate([qkv_shard, jnp.pad(line, ((0, tall - band - 1), (0, 0)))], axis=0)
    got_one = lax.all_gather(shard_one, OWNER, axis=0, tiled=True).reshape(mp, dp, tall, wide)
    x_bf = lax.all_to_all(frames, "mb", 0, 0, tiled=True).reshape(rows, width)
    shard_two = jnp.concatenate([w_up, w_down.T, w_out.T], axis=1)
    shard_two = lax.optimization_barrier((shard_two, got_one))
    got_one = shard_two[1]
    got_two = lax.all_gather(shard_two[0], OWNER, axis=0, tiled=True).reshape(mp, width, 2 * ff + head_cols)
    g_bf = lax.all_to_all(cotangent, "mb", 0, 0, tiled=True).reshape(rows, width)

    weight_qkv = got_one[:, :, :band].reshape(mp, width, wide)
    lines = got_one[:, :, band].astype(f32)
    cuts = []
    at = 0
    for size in small_sizes:
        cuts.append(lines[:, :, at : at + size])
        at += size
    bias_qv = cuts[0].reshape(mp, dp, 2, -1).transpose(2, 0, 1, 3).reshape(2, mp, head_cols)
    bias_up = cuts[1].reshape(mp, ff)
    gain_rows = cuts[2].reshape(mp, dp, 2, -1).transpose(2, 1, 0, 3).reshape(2, width)
    bias_rows = cuts[3].reshape(mp, dp, 4, -1).transpose(2, 1, 0, 3).reshape(4, width)
    weight_up = got_two[:, :, :ff]
    weight_down = got_two[:, :, ff : 2 * ff]
    weight_out = got_two[:, :, 2 * ff :]

    clip_row = lax.dynamic_index_in_dim(clip_ids, lax.axis_index("mb"), 0, keepdims=False)
    by_source = clip_row.reshape(mbs, parts, mp, share)
    if parts == 2:
        halves = by_source.reshape(2, 2, parts, mp, share)
        pair_flip = ((jnp.arange(mp) // 2 + my_part) % 2 == 1)[None, None, :, None]
        qid = jnp.where(pair_flip, halves[:, 1], halves[:, 0])
    else:
        lined = by_source.transpose(1, 2, 0, 3).reshape(parts, mp, rows)
        qid = lax.dynamic_slice_in_dim(lined, my_part * piece, piece, 2)
        qid = qid.reshape(parts, mp, 2, half).transpose(2, 0, 1, 3)
    qid = qid.reshape(-1)
    tiles = qid.reshape(-1, QT)
    lowest = jnp.min(tiles, axis=1)[:, None]
    highest = jnp.max(tiles, axis=1)[:, None]
    span = jnp.stack(
        [
            jnp.sum(clip_row[None] < lowest, axis=1, dtype=jnp.int32),
            jnp.sum(clip_row[None] <= highest, axis=1, dtype=jnp.int32),
        ]
    )
    block = min(seq, 4608)
    qid = qid[:, None]
    kid = clip_row.reshape(seq // block, 1, block)

    def to_parts(q):
        if parts == 2:
            q = q.reshape(mp, 2, 2, share, head_cols)
            q = jnp.where(flip, q[:, :, ::-1], q).transpose(2, 0, 3, 1, 4)
        else:
            q = q.reshape(mp, parts, 2, half, head_cols).transpose(1, 0, 3, 2, 4)
        return q.reshape(parts, mp, half, 2 * head_cols)

    def from_parts(q):
        q = q.reshape(parts, mp, half, 2, head_cols)
        if parts == 2:
            q = q.transpose(1, 3, 0, 2, 4)
            q = jnp.where(flip, q[:, :, ::-1], q)
        else:
            q = q.transpose(1, 0, 3, 2, 4)
        return q.reshape(mp, rows, head_cols)

    def to_tiles(q):
        return q.reshape(parts, mp, half, 2, head_cols).transpose(3, 0, 1, 2, 4).reshape(-1, head_cols)

    def from_tiles(q):
        return q.reshape(2, parts, mp, half, head_cols).transpose(1, 2, 3, 0, 4).reshape(parts, mp, half, 2 * head_cols)

    def swap(a):
        return lax.all_to_all(a.reshape((parts * mp,) + a.shape[2:]), PLANE, 0, 0, tiled=True).reshape(a.shape)

    x = x_bf.astype(f32)
    hat_one, inv_one = standard(x)
    h1 = (hat_one * gain_rows[0] + bias_rows[0]).astype(bf16)
    bias_q = bias_qv[0]
    bias_v = bias_qv[1].reshape(mp, heads, 1, HD)
    bias_kv = jnp.concatenate([jnp.zeros_like(bias_v), bias_v], axis=2).reshape(mp, 2 * head_cols)
    bias_all = jnp.concatenate([bias_q, bias_kv], axis=1)
    proj = jnp.stack([(dot(h1, weight_qkv[m]) + bias_all[m]).astype(bf16) for m in range(mp)])
    kv_part = jnp.broadcast_to(proj[None, :, :, head_cols:], (parts, mp, rows, 2 * head_cols))
    sent = jnp.concatenate([to_parts(proj[:, :, :head_cols]), kv_part], axis=2)
    came = swap(sent)
    q_tiles = to_tiles(came[:, :, :half])
    kv_seq = (
        came[:, :, half:].reshape(parts, mp, mbs, share, 2 * head_cols).transpose(2, 0, 1, 3, 4).reshape(seq, 2 * head_cols)
    )
    att_tiles, lse = attend(span, q_tiles, qid, kid, kv_seq, heads, block)
    att = from_parts(swap(from_tiles(att_tiles)))
    mixed = x + bias_rows[1]
    for m in range(mp):
        mixed = mixed + dot(att[m], weight_out[m], NT)
    hat_two, inv_two = standard(mixed)
    h2 = (hat_two * gain_rows[1] + bias_rows[2]).astype(bf16)
    g = g_bf.astype(f32)
    result = mixed + bias_rows[3]
    grad_two = jnp.zeros((rows, width), f32)
    ups, downs, bups = [], [], []
    for m in range(mp):
        u = dot(h2, weight_up[m]) + bias_up[m]
        act, pull = jax.vjp(gelu_exact, u)
        act = act.astype(bf16)
        result = result + dot(act, weight_down[m], NT)
        du = pull(dot(g_bf, weight_down[m]))[0].astype(bf16)
        grad_two = grad_two + dot(du, weight_up[m], NT)
        ups.append(dot(h2, du, TN).astype(bf16))
        downs.append(dot(g_bf, act, TN).astype(bf16))
        bups.append(jnp.sum(du, axis=0, dtype=f32))
    output = lax.all_to_all(result.astype(bf16).reshape(mbs, share, width), "mb", 0, 0, tiled=True)

    dr1 = g + norm_pull(grad_two, hat_two, inv_two, gain_rows[1])
    drb = dr1.astype(bf16)
    datt = jnp.stack([dot(drb, weight_out[m]).astype(bf16) for m in range(mp)])
    datt_tiles = to_tiles(swap(to_parts(datt)))
    outs = [dot(drb, att[m], TN).astype(bf16) for m in range(mp)]
    grads_two = jnp.stack([jnp.concatenate([ups[m], downs[m], outs[m]], axis=1) for m in range(mp)])
    mine_two = lax.psum_scatter(
        grads_two.reshape(mp * width, 2 * ff + head_cols), OWNER, scatter_dimension=0, tiled=True
    ).astype(f32)

    dq_tiles, dkv_seq = attend_pull(span, q_tiles, qid, kid, kv_seq, datt_tiles, att_tiles, lse, heads, block)
    dkv = dkv_seq.reshape(mbs, parts, mp, share, 2 * head_cols).transpose(1, 2, 0, 3, 4).reshape(parts, mp, rows, 2 * head_cols)
    back = swap(jnp.concatenate([from_tiles(dq_tiles), dkv], axis=2))
    dq = from_parts(back[:, :, :half])
    dkv = jnp.sum(back[:, :, half:], axis=0, dtype=f32).astype(bf16)
    dproj = jnp.concatenate([dq, dkv], axis=2)
    grad_one = jnp.zeros((rows, width), f32)
    for m in range(mp):
        grad_one = grad_one + dot(dproj[m], weight_qkv[m], NT)
    dx = (dr1 + norm_pull(grad_one, hat_one, inv_one, gain_rows[0])).astype(bf16)
    frames_grad = lax.all_to_all(dx.reshape(mbs, share, width), "mb", 0, 0, tiled=True)

    grads_qkv = jnp.stack([dot(h1, dproj[m], TN).astype(bf16) for m in range(mp)])
    col_sums = jnp.sum(dproj, axis=1, dtype=f32)
    dbq = col_sums[:, :head_cols].reshape(mp, dp, 1, -1)
    dbv = col_sums[:, head_cols:].reshape(mp, heads, 2, HD)[:, :, 1].reshape(mp, dp, 1, -1)
    dbup = jnp.stack(bups).reshape(mp, dp, -1)
    dgains = jnp.stack([jnp.sum(grad_one * hat_one, axis=0), jnp.sum(grad_two * hat_two, axis=0)])
    dbiases = jnp.stack(
        [jnp.sum(grad_one, axis=0), jnp.sum(dr1, axis=0), jnp.sum(grad_two, axis=0), jnp.sum(g, axis=0)]
    )

    def by_owner(a):
        return a.reshape(a.shape[0], dp, mp, -1).transpose(2, 1, 0, 3).reshape(mp, dp, -1)

    small = jnp.concatenate(
        [jnp.concatenate([dbq, dbv], axis=2).reshape(mp, dp, -1), dbup, by_owner(dgains), by_owner(dbiases)], axis=2
    )
    small = jnp.pad(small, ((0, 0), (0, 0), (0, wide - small.shape[2])))[:, :, None].astype(bf16)
    small = jnp.pad(small, ((0, 0), (0, 0), (0, tall - band - 1), (0, 0)))
    grads_one = jnp.concatenate([grads_qkv.reshape(mp, dp, band, wide), small], axis=2)
    mine_one = lax.psum_scatter(
        grads_one.reshape(mp * dp * tall, wide), OWNER, scatter_dimension=0, tiled=True
    ).astype(f32)

    kv_mine = mine_one[:band, head_cols:].reshape(band, heads, 2, HD)
    grad_qkv = jnp.stack(
        [
            mine_one[:band, :head_cols],
            kv_mine[:, :, 0].reshape(band, head_cols),
            kv_mine[:, :, 1].reshape(band, head_cols),
        ],
        axis=1,
    )
    small_mine = mine_one[band]
    pieces = []
    at = 0
    for size, like in zip(small_sizes, smalls):
        pieces.append(small_mine[at : at + size].reshape(like.shape))
        at += size
    return (
        output,
        frames_grad,
        grad_qkv,
        pieces[0],
        mine_two[:, 2 * ff :].T,
        mine_two[:, :ff],
        pieces[1],
        mine_two[:, ff : 2 * ff].T,
        pieces[2],
        pieces[3],
    )


def solution(mesh):
    mbs = 4
    split = Mesh(
        mesh.devices.reshape(mbs, mesh.shape["dp"] // mbs, mesh.shape["mp"]), ("mb", "part", "mp")
    )
    dp = ("mb", "part")
    placed = (
        P(None, ALL, None),
        P(),
        P(dp, None, "mp"),
        P(None, "mp", dp),
        P("mp", dp),
        P(dp, "mp"),
        P("mp", dp),
        P("mp", dp),
        P(None, ALL),
        P(None, ALL),
        P(None, ALL, None),
    )
    return jax.shard_map(
        local,
        mesh=split,
        in_specs=placed,
        out_specs=(
            P(None, ALL, None),
            P(None, ALL, None),
            P(dp, None, "mp"),
            P(None, "mp", dp),
            P("mp", dp),
            P(dp, "mp"),
            P("mp", dp),
            P("mp", dp),
            P(None, ALL),
            P(None, ALL),
        ),
        check_vma=False,
    )
```

time: 3580 us -> 998 us (0.28)
  blocking collectives: 1450 us -> 49.1 us
  waiting for transfers between devices: 1050 us -> 401 us
  other arithmetic: 347 us -> 49.2 us
  matrix products: 374 us -> 95.2 us
  Pallas kernels: 0 us -> 158 us
  starting transfers between devices: 122 us -> 69.1 us
  local copies, waits for them, and re-layouts: 192 us -> 155 us
    all_gather x48 -> x0, blocking collectives: 1300 us -> none  [the longest x8 321 us: fetch_weights(): lax.all_gather(gains, ('dp', 'mp'), axis=1, tiled=True)]
    all_gather x16 -> x2, waiting for transfers between devices: 434 us -> 65 us  [the longest x1 65 us: local(): lax.all_gather(shard_one, OWNER, axis=0, tiled=True)]
    reduce_scatter x19 -> x1, waiting for transfers between devices: 451 us -> 142 us  [local(): lax.psum_scatter(grads_two.reshape(mp * width, 2 * ff + head_cols), OWNER...]
    dot_general x116 -> x48, matrix products: 370 us -> 95.2 us  [dot(): return lax.dot_general(a, b, dims, preferred_element_type=f32)]
    convert_element_type x40 -> x8, other arithmetic: 203 us -> 6.52 us  [the longest x1 3.01 us: local(): (dr1 + norm_pull(grad_one, hat_one, inv_one, gain_rows[0])).astype(bf16)]
    pallas_call x0 -> x2, Pallas kernels: none -> 158 us  [the longest x1 90.3 us: attend(): pl.pallas_call(functools.partial(attend_kernel, heads=heads, block=block)...]
    all_to_all x0 -> x6, waiting for transfers between devices: none -> 151 us  [the longest x3 97.8 us: swap(): lax.all_to_all(a.reshape((parts * mp,) + a.shape[2:]), PLANE, 0, 0, tiled...]
    ppermute x48 -> x0, starting transfers between devices: 120 us -> none  [passed_along(): return lax.ppermute(array, axis, pairs)]
  transfers between devices with their start and end apart: 85 -> 10, of which waited for: 52 -> 8; matrix products, arithmetic and copies ran while one was open for 8% -> 17% of each run, Pallas kernels for 0% -> 9%
where the time goes in v1:
time: 998 us; the launch traced here: 992 us
  waiting for transfers between devices  401 us (40%)
  Pallas kernels  158 us (16%)
  local copies, waits for them, and re-layouts  155 us (16%)
  matrix products  95.2 us (10%)
  starting transfers between devices  69.1 us (7%)
  other arithmetic  49.2 us (5%)
  blocking collectives  49.1 us (5%)
  between operations  15.5 us (2%)
    reduce_scatter x1, waiting for transfers between devices, local(): lax.psum_scatter(grads_two.reshape(mp * width, 2 * ff + head_cols), OWNER...  142 us
    all_to_all x3, waiting for transfers between devices, swap(): lax.all_to_all(a.reshape((parts * mp,) + a.shape[2:]), PLANE, 0, 0, tiled...  97.8 us
    dot_general x48, matrix products, dot(): return lax.dot_general(a, b, dims, preferred_element_type=f32)  95.2 us
    pallas_call x1, Pallas kernels, attend(): pl.pallas_call(functools.partial(attend_kernel, heads=heads, block=block)...  90.3 us
    pallas_call x1, Pallas kernels, attend_pull(): pl.pallas_call(functools.partial(pull_kernel, heads=heads, block=block),...  67.9 us
    all_gather x1, waiting for transfers between devices, local(): lax.all_gather(shard_one, OWNER, axis=0, tiled=True)  65 us
    unnamed x5, waiting for transfers between devices  43.7 us
    all_to_all x1, blocking collectives, local(): lax.all_to_all(dx.reshape(mbs, share, width), 'mb', 0, 0, tiled=True)  32.4 us
  transfers between devices with their start and end apart: 10, of which 8 were waited for; matrix products, arithmetic and copies ran while one was open for 17% of the time, Pallas kernels for 9%

profile of v1, /device:TPU:0, one launch (start us, length us, event | category | flops | bytes accessed | tf_op | source)
XLA Modules:
  0.0 992.3 jit_solution(17300098191647959835)
XLA Ops:
  13.6 65.0 %all-gather.3.cloned.1.call-done = bf16[3584,576]{1,0:T(8,128)(2,1)} async-done(((bf16[112,576]{1,0:T(8,128)(2,1)}), bf16[3584,576]{1,0:T(8,128)(2,1)}) %all-gather.3.cloned.1.call-update) | async-done | bytes 4128784 | tf_op jit(solution)/shard_map/all_gather | solution.py:272
  78.6 8.3 copy.302
  90.6 30.2 %all-to-all-done = bf16[4,144,768]{2,1,0:T(8,128)(2,1)S(1)} async-done(((bf16[4,144,768]{2,1,0:T(8,128)(2,1)}), bf16[4,144,768]{2,1,0:T(8,128)(2,1)S(1)}, u32[]{:S(2)}, u32[]{:S(2)}) %all-to-all-start) | async-done | bytes 884768 | tf_op jit(solution)/shard_map/all_to_all | solution.py:273
  121.5 9.4 copy.251
  174.0 44.3 %all-to-all-done.1 = bf16[8,720,384]{2,1,0:T(8,128)(2,1)} async-done(((bf16[8,720,384]{2,1,0:T(8,128)(2,1)}), bf16[8,720,384]{2,1,0:T(8,128)(2,1)}, u32[]{:S(2)}, u32[]{:S(2)}) %all-to-all-start.1) | async-done | bytes 4423712 | tf_op jit(solution)/shard_map/all_to_all | solution.py:343
  229.8 90.3 %attend.1 = (bf16[2304,192]{1,0:T(8,128)(2,1)}, f32[3,2304,1]{2,1,0:T(8,128)}) custom-call(s32[2,8]{1,0:T(2,128)} %pad_add_fusion.span_ref, bf16[2304,192]{1,0:T(8,128)(2,1)} %bitcast.397, s32[2304,1]{1,0:T(8,128)} %select_n.78.qid_ref, s32[1,1,4608]{2,1,0:T(1,128)} %get-tuple-element.133.kid_ref, bf16[4608,384]{1,0:T(8,128)(2,1)} %bitcast.383), custom_call_target="tpu_custom_call" | custom-call | tf_op jit(solution)/shard_map/attend/pallas_call | solution.py:105
  324.1 9.3 all-to-all-start.2
  337.8 9.2 all-to-all-done.2
  347.9 24.5 %all-to-all-start.4 = ((bf16[4,144,768]{2,1,0:T(8,128)(2,1)}), bf16[4,144,768]{2,1,0:T(8,128)(2,1)S(1)}, u32[]{:S(2)}, u32[]{:S(2)}) async-start(bf16[4,144,768]{2,1,0:T(8,128)(2,1)} %param.21), calls=%async_computation.4 | async-start | bytes 1769472 | tf_op jit(solution)/shard_map/all_to_all | solution.py:278
  385.9 7.3 multiply_convert_fusion.1
  393.2 7.0 multiply_convert_fusion.2
  400.2 7.0 multiply_convert_fusion.3
  407.2 7.5 multiply_convert_fusion
  455.4 16.7 %all_to_all.40 = bf16[8,144,384]{2,1,0:T(8,128)(2,1)} all-to-all(bf16[8,144,384]{2,1,0:T(8,128)(2,1)S(1)} %reshape_reshape.19), channel_id=1, replica_groups=mesh['mb'=4,'part'=2,'mp'=4] {'part','mp'}, dimensions={0} | all-to-all | bytes 1769472 | tf_op jit(solution)/shard_map/all_to_all | solution.py:343
  478.7 67.9 %attend_pull.1 = (bf16[2304,192]{1,0:T(8,128)(2,1)}, bf16[4608,384]{1,0:T(8,128)(2,1)}) custom-call(s32[2,8]{1,0:T(2,128)} %pad_add_fusion.span_ref, bf16[2304,192]{1,0:T(8,128)(2,1)} %bitcast.398, s32[2304,1]{1,0:T(8,128)} %select_n.78.qid_ref, s32[1,1,4608]{2,1,0:T(1,128)} %get-tuple-element.133.kid_ref, bf16[4608,384]{1,0:T(8,128)(2,1)} %bitcast.384, ...), custom_call_target="tpu_custom_call" | custom-call | tf_op jit(solution)/shard_map/attend_pull/pallas_call | solution.py:197
  560.7 7.2 all-to-all-start.6
  575.3 44.2 %all-to-all-done.6 = bf16[8,720,384]{2,1,0:T(8,128)(2,1)} async-done(((bf16[8,720,384]{2,1,0:T(8,128)(2,1)}), bf16[8,720,384]{2,1,0:T(8,128)(2,1)}, u32[]{:S(2)}, u32[]{:S(2)}) %all-to-all-start.6) | async-done | bytes 4423712 | tf_op jit(solution)/shard_map/all_to_all | solution.py:343
  681.1 5.3 pad_maximum_fusion
  686.4 14.0 %copy.297 = bf16[4,768,1728]{2,1,0:T(8,128)(2,1)} copy(bf16[4,768,1728]{1,2,0:T(8,128)(2,1)} %pad_maximum_fusion) | data formatting | bytes 21233664 | tf_op jit(solution)/shard_map/stack | solution.py:388
  711.3 19.7 %all-to-all-start.3 = ((bf16[4,144,768]{2,1,0:T(8,128)(2,1)}), bf16[4,144,768]{2,1,0:T(8,128)(2,1)S(1)}, u32[]{:S(2)}, u32[]{:S(2)}) async-start(bf16[4,144,768]{2,1,0:T(8,128)(2,1)} %bitcast.57), calls=%async_computation.3 | async-start | bytes 1769472 | tf_op jit(solution)/shard_map/all_to_all | solution.py:381
  734.7 22.9 %all-to-all-done.3 = bf16[4,144,768]{2,1,0:T(8,128)(2,1)S(1)} async-done(((bf16[4,144,768]{2,1,0:T(8,128)(2,1)}), bf16[4,144,768]{2,1,0:T(8,128)(2,1)S(1)}, u32[]{:S(2)}, u32[]{:S(2)}) %all-to-all-start.3) | async-done | bytes 884768 | tf_op jit(solution)/shard_map/all_to_all | solution.py:381
  757.6 32.4 %all_to_all.41 = bf16[4,144,768]{2,1,0:T(8,128)(2,1)S(1)} all-to-all(bf16[4,144,768]{2,1,0:T(8,128)(2,1)} %bitcast.430), channel_id=1, replica_groups=mesh['mb'=4,'part'=2,'mp'=4] {'mb'}, dimensions={0} | all-to-all | bytes 1769472 | tf_op jit(solution)/shard_map/all_to_all | solution.py:403
  789.9 43.6 %reduce-scatter.7.cloned.1.call-done = bf16[112,576]{1,0:T(8,128)(2,1)} async-done(((bf16[3584,576]{1,0:T(8,128)(2,1)}), bf16[112,576]{1,0:T(8,128)(2,1)}) %reduce-scatter.7.cloned.1.call-update) | async-done | bytes 129040
  838.6 141.8 %reduce-scatter.5.cloned.1.call-done = bf16[96,1728]{1,0:T(8,128)(2,1)} async-done(((bf16[3072,1728]{1,0:T(8,128)(2,1)}), bf16[96,1728]{1,0:T(8,128)(2,1)}) %reduce-scatter.5.cloned.1.call-update) | async-done | bytes 331792 | tf_op jit(solution)/shard_map/reduce_scatter | solution.py:389
  (420 shorter events, 241.7 us)
Async XLA Ops:
  7.2 71.4 %all-gather.3.cloned.1.call-start = ((), (), s32[]{:S(2)}) async-start(), calls=%async_computation.10 | async-start | bytes 4730880 | tf_op jit(solution)/shard_map/all_gather | solution.py:272
  12.7 366.0 %all-gather.5.cloned.1.call-start = ((), (), s32[]{:S(2)}) async-start(), calls=%async_computation.11 | async-start | bytes 11354112 | tf_op jit(solution)/shard_map/all_gather | solution.py:277
  87.0 33.8 %all-to-all-start = ((bf16[4,144,768]{2,1,0:T(8,128)(2,1)}), bf16[4,144,768]{2,1,0:T(8,128)(2,1)S(1)}, u32[]{:S(2)}, u32[]{:S(2)}) async-start(bf16[4,144,768]{2,1,0:T(8,128)(2,1)} %param.11), calls=%async_computation | async-start | bytes 1769472 | tf_op jit(solution)/shard_map/all_to_all | solution.py:273
  121.0 26.5 %copy-start.42 = (f32[4,144]{1,0:T(4,128)}, f32[4,144]{1,0:T(4,128)S(1)}, u32[]{:S(2)}) copy-start(f32[4,144]{1,0:T(4,128)S(1)} %broadcast_multiply_fusion.5) | copy-start | bytes 6916
  121.5 26.1 %copy-start.49 = (f32[4,144]{1,0:T(4,128)}, f32[4,144]{1,0:T(4,128)S(1)}, u32[]{:S(2)}) copy-start(f32[4,144]{1,0:T(4,128)S(1)} %add_rsqrt_fusion.1) | copy-start | bytes 6916
  162.0 56.3 %all-to-all-start.1 = ((bf16[8,720,384]{2,1,0:T(8,128)(2,1)}), bf16[8,720,384]{2,1,0:T(8,128)(2,1)}, u32[]{:S(2)}, u32[]{:S(2)}) async-start(bf16[8,720,384]{2,1,0:T(8,128)(2,1)} %pad_maximum_fusion.2), calls=%async_computation.1 | async-start | bytes 8847360 | tf_op jit(solution)/shard_map/all_to_all | solution.py:343
  322.6 12.3 %copy-start.47 = (f32[1,8,4,24]{3,0,1,2:T(1,128)S(1)}, f32[1,8,4,24]{3,0,1,2:T(1,128)}, u32[]{:S(2)}) copy-start(f32[1,8,4,24]{3,0,1,2:T(1,128)} %get-tuple-element.138) | copy-start | bytes 9220
  322.6 12.4 %copy-start.46 = (f32[1,8,4,24]{3,0,1,2:T(1,128)S(1)}, f32[1,8,4,24]{3,0,1,2:T(1,128)}, u32[]{:S(2)}) copy-start(f32[1,8,4,24]{3,0,1,2:T(1,128)} %get-tuple-element.136) | copy-start | bytes 9220
  322.6 13.1 %copy-start.44 = (f32[1,8,4,24]{3,0,1,2:T(1,128)S(1)}, f32[1,8,4,24]{3,0,1,2:T(1,128)}, u32[]{:S(2)}) copy-start(f32[1,8,4,24]{3,0,1,2:T(1,128)} %get-tuple-element.139) | copy-start | bytes 9220
  324.1 22.9 %all-to-all-start.2 = ((bf16[8,144,384]{2,1,0:T(8,128)(2,1)}), bf16[8,144,384]{2,1,0:T(8,128)(2,1)S(1)}, u32[]{:S(2)}, u32[]{:S(2)}) async-start(bf16[8,144,384]{2,1,0:T(8,128)(2,1)} %reshape_reshape.17), calls=%async_computation.2 | async-start | bytes 1769472 | tf_op jit(solution)/shard_map/all_to_all | solution.py:343
  347.9 66.9 %all-to-all-start.4 = ((bf16[4,144,768]{2,1,0:T(8,128)(2,1)}), bf16[4,144,768]{2,1,0:T(8,128)(2,1)S(1)}, u32[]{:S(2)}, u32[]{:S(2)}) async-start(bf16[4,144,768]{2,1,0:T(8,128)(2,1)} %param.21), calls=%async_computation.4 | async-start | bytes 1769472 | tf_op jit(solution)/shard_map/all_to_all | solution.py:278
  384.8 51.4 %copy-start = (f32[576,768]{1,0:T(8,128)}, f32[576,768]{1,0:T(8,128)S(1)}, u32[]{:S(2)}) copy-start(f32[576,768]{1,0:T(8,128)S(1)} %get-tuple-element.144) | copy-start | bytes 5308420
  385.9 21.4 %copy-start.35 = (bf16[576,768]{1,0:T(8,128)(2,1)}, bf16[576,768]{1,0:T(8,128)(2,1)S(1)}, u32[]{:S(2)}) copy-start(bf16[576,768]{1,0:T(8,128)(2,1)S(1)} %add_convert_fusion.2) | copy-start | bytes 2654212
  385.9 7.3 copy-start.60
  414.8 153.3 %copy-start.6 = (bf16[4,144,768]{2,1,0:T(8,128)(2,1)}, bf16[4,144,768]{2,1,0:T(8,128)(2,1)S(1)}, u32[]{:S(2)}) copy-start(bf16[4,144,768]{2,1,0:T(8,128)(2,1)S(1)} %all-to-all-done.4) | copy-start | bytes 2654212
  414.8 10.7 %slice-start = ((s8[11010048]{0:T(1024)(128)(4,1)}), s8[4194304]{0:T(1024)(128)(4,1)S(1)}, s32[]{:S(2)}) async-start(s8[11010048]{0:T(1024)(128)(4,1)} %bitcast.446), calls=%async_computation.14 | async-start | bytes 8388608
  414.8 10.7 %slice-start.1 = ((s8[11010048]{0:T(1024)(128)(4,1)}), s8[4194304]{0:T(1024)(128)(4,1)S(1)}, s32[]{:S(2)}) async-start(s8[11010048]{0:T(1024)(128)(4,1)} %bitcast.446), calls=%async_computation.15 | async-start | bytes 8388608
  560.7 7.4 copy-start.43
  560.7 58.9 %all-to-all-start.6 = ((bf16[8,720,384]{2,1,0:T(8,128)(2,1)}), bf16[8,720,384]{2,1,0:T(8,128)(2,1)}, u32[]{:S(2)}, u32[]{:S(2)}) async-start(bf16[8,720,384]{2,1,0:T(8,128)(2,1)} %pad_maximum_fusion.3), calls=%async_computation.6 | async-start | bytes 8847360 | tf_op jit(solution)/shard_map/all_to_all | solution.py:343
  567.9 265.7 %reduce-scatter.7.cloned.1.call-start = ((), (), s32[]{:S(2)}) async-start(), calls=%async_computation.13 | async-start | bytes 4730880
  667.5 312.9 %reduce-scatter.5.cloned.1.call-start = ((), (), s32[]{:S(2)}) async-start(), calls=%async_computation.12 | async-start | bytes 11354112 | tf_op jit(solution)/shard_map/reduce_scatter | solution.py:389
  711.3 20.4 %copy-start.53 = (f32[576]{0:T(1024)S(1)}, f32[576]{0:T(1024)}, u32[]{:S(2)}) copy-start(f32[576]{0:T(1024)} %get-tuple-element.90) | copy-start | bytes 6916
  711.3 20.4 %copy-start.5 = (f32[576,768]{1,0:T(8,128)S(1)}, f32[576,768]{1,0:T(8,128)}, u32[]{:S(2)}) copy-start(f32[576,768]{1,0:T(8,128)} %copy-done.4) | copy-start | bytes 5308420
  711.3 46.3 %all-to-all-start.3 = ((bf16[4,144,768]{2,1,0:T(8,128)(2,1)}), bf16[4,144,768]{2,1,0:T(8,128)(2,1)S(1)}, u32[]{:S(2)}, u32[]{:S(2)}) async-start(bf16[4,144,768]{2,1,0:T(8,128)(2,1)} %bitcast.57), calls=%async_computation.3 | async-start | bytes 1769472 | tf_op jit(solution)/shard_map/all_to_all | solution.py:381
  (75 other events, 186.7 us)
Sparse Core Ops, SparseCore 0:
  12.8 65.7 all-gather.2
  87.1 98.6 all-gather.4
  667.6 165.8 reduce-scatter.6
  839.4 141.0 reduce-scatter.4

commit v2 on v1

--- a/solution.py
+++ b/solution.py
@@ -28,12 +28,21 @@
 
 
 def tile_span(span_ref, tile, base, block):
-    first = jnp.maximum(span_ref[0, tile] - base, 0) // KT
-    last = (jnp.minimum(span_ref[1, tile] - base, block) + (KT - 1)) // KT
-    return first, jnp.maximum(last, first)
-
-
-def attend_kernel(span_ref, q_ref, qid_ref, kid_ref, kv_ref, att_ref, lse_ref, m_ref, l_ref, acc_ref, *, heads, block):
+    first = jnp.clip(span_ref[0, tile] - base, 0, block) // 128 * 128
+    last = jnp.clip(span_ref[1, tile] - base, 0, block)
+    count = jnp.maximum(last - first + (KT - 1), 0) // KT
+    return jnp.minimum(first, block - count * KT), count
+
+
+def twice(a):
+    return jnp.concatenate([a, a], axis=1)
+
+
+def spread(column):
+    return jnp.broadcast_to(column, (column.shape[0], 128))
+
+
+def attend_kernel(span_ref, q_ref, qid_ref, kid_ref, kv_ref, att_ref, lse_ref, m_ref, acc_ref, s_ref, vo_ref, *, heads, block):
     step = pl.program_id(0)
     steps = pl.num_programs(0)
     tiles = q_ref.shape[0] // QT
@@ -41,57 +50,65 @@
     @pl.when(step == 0)
     def _():
         m_ref[...] = jnp.full(m_ref.shape, MASKED, f32)
-        l_ref[...] = jnp.zeros(l_ref.shape, f32)
         acc_ref[...] = jnp.zeros(acc_ref.shape, f32)
+
+    def fill(i, _):
+        chunk = pl.ds(pl.multiple_of(i * KT, KT), KT)
+        ones = jnp.ones((KT, HD), bf16)
+        for h in range(heads):
+            vo_ref[chunk, h * 128 : (h + 1) * 128] = jnp.concatenate(
+                [ones, kv_ref[chunk, h * 128 + HD : (h + 1) * 128]], axis=1
+            )
+        return 0
+
+    lax.fori_loop(0, block // KT, fill, 0)
 
     def one_tile(tile, _):
         rows = pl.ds(pl.multiple_of(tile * QT, QT), QT)
         q_all = q_ref[rows, :]
-        qid = qid_ref[rows, :]
+        blank = jnp.zeros((QT, HD), bf16)
         queries = [
-            jnp.concatenate(
-                [q_all[:, h * HD : (h + 1) * HD] * bf16(SCALE), jnp.zeros((QT, HD), bf16)], axis=1
-            )
+            jnp.concatenate([q_all[:, h * HD : (h + 1) * HD] * bf16(SCALE), blank], axis=1)
             for h in range(heads)
         ]
-        first, last = tile_span(span_ref, tile, step * block, block)
-
-        def body(kt, state):
-            cols = pl.ds(pl.multiple_of(kt * KT, KT), KT)
-            same = qid == kid_ref[0, :, cols]
+        start, count = tile_span(span_ref, tile, step * block, block)
+
+        def score(i, tops):
+            cols = pl.ds(pl.multiple_of(start + i * KT, 128), KT)
+            kept = pl.ds(pl.multiple_of(i * KT, KT), KT)
+            same = twice(qid_ref[rows, :]) == kid_ref[0, :, cols]
             out = []
             for h in range(heads):
-                m, l, acc = state[h]
-                kv = kv_ref[cols, h * 128 : (h + 1) * 128]
-                s = jnp.where(same, dot(queries[h], kv, NT), MASKED)
-                m_new = jnp.maximum(m, jnp.max(s, axis=1, keepdims=True))
-                p = jnp.exp(s - m_new)
-                keep = jnp.exp(m - m_new)
-                out.append(
-                    (
-                        m_new,
-                        l * keep + jnp.sum(p, axis=1, keepdims=True),
-                        acc * keep + dot(p.astype(bf16), kv),
-                    )
-                )
+                s = jnp.where(same, dot(queries[h], kv_ref[cols, h * 128 : (h + 1) * 128], NT), MASKED)
+                s_ref[h, :, kept] = s
+                out.append(jnp.maximum(tops[h], jnp.maximum(s[:, :128], s[:, 128:])))
             return tuple(out)
 
-        state = tuple(
-            (m_ref[h, rows, :], l_ref[h, rows, :], acc_ref[h, rows, :]) for h in range(heads)
-        )
-        state = lax.fori_loop(first, last, body, state)
+        tops = tuple(jnp.full((QT, 128), MASKED, f32) for _ in range(heads))
+        tops = lax.fori_loop(0, count, score, tops)
         for h in range(heads):
-            m_ref[h, rows, :] = state[h][0]
-            l_ref[h, rows, :] = state[h][1]
-            acc_ref[h, rows, :] = state[h][2]
+            old = m_ref[h, rows, :]
+            new = jnp.maximum(old, spread(jnp.max(tops[h], axis=1, keepdims=True)))
+            m_ref[h, rows, :] = new
+            acc_ref[h, rows, :] = acc_ref[h, rows, :] * jnp.exp(old - new)
+
+        def weigh(i, _):
+            cols = pl.ds(pl.multiple_of(start + i * KT, 128), KT)
+            kept = pl.ds(pl.multiple_of(i * KT, KT), KT)
+            for h in range(heads):
+                p = jnp.exp(s_ref[h, :, kept] - twice(m_ref[h, rows, :]))
+                acc_ref[h, rows, :] += dot(p.astype(bf16), vo_ref[cols, h * 128 : (h + 1) * 128])
+            return 0
+
+        lax.fori_loop(0, count, weigh, 0)
 
         @pl.when(step == steps - 1)
         def _():
             outs = []
             for h in range(heads):
-                m, l, acc = state[h]
-                outs.append((acc / l)[:, HD:])
-                lse_ref[h, rows, :] = m + jnp.log(l)
+                acc = acc_ref[h, rows, :]
+                outs.append(acc[:, HD:] / acc[:, :HD])
+                lse_ref[h, rows, :] = m_ref[h, rows, :] + jnp.log(spread(acc[:, :1]))
             att_ref[rows, :] = jnp.concatenate(outs, axis=1).astype(bf16)
 
         return 0
@@ -115,23 +132,24 @@
             ],
             out_specs=[
                 pl.BlockSpec(q.shape, whole),
-                pl.BlockSpec((heads, rows, 1), lambda s, _: (0, 0, 0)),
+                pl.BlockSpec((heads, rows, 128), lambda s, _: (0, 0, 0)),
             ],
             scratch_shapes=[
-                pltpu.VMEM((heads, rows, 1), f32),
-                pltpu.VMEM((heads, rows, 1), f32),
                 pltpu.VMEM((heads, rows, 128), f32),
+                pltpu.VMEM((heads, rows, 128), f32),
+                pltpu.VMEM((heads, QT, block), f32),
+                pltpu.VMEM((block, kv.shape[1]), bf16),
             ],
         ),
         out_shape=[
             jax.ShapeDtypeStruct(q.shape, bf16),
-            jax.ShapeDtypeStruct((heads, rows, 1), f32),
+            jax.ShapeDtypeStruct((heads, rows, 128), f32),
         ],
         name="attend",
     )(span, q, qid, kid, kv)
 
 
-def pull_kernel(span_ref, q_ref, qid_ref, kid_ref, kv_ref, datt_ref, att_ref, lse_ref, dq_ref, dkv_ref, dq_acc, dkv_acc, *, heads, block):
+def pull_kernel(span_ref, q_ref, qid_ref, kid_ref, kv_ref, datt_ref, att_ref, lse_ref, dq_ref, dkv_ref, dq_acc, dkv_acc, delta_ref, stack_ref, *, heads, block):
     step = pl.program_id(0)
     steps = pl.num_programs(0)
     tiles = q_ref.shape[0] // QT
@@ -146,43 +164,36 @@
         rows = pl.ds(pl.multiple_of(tile * QT, QT), QT)
         q_all = q_ref[rows, :]
         d_all = datt_ref[rows, :]
-        qid = qid_ref[rows, :]
         both = d_all.astype(f32) * att_ref[rows, :].astype(f32)
         blank = jnp.zeros((QT, HD), bf16)
-        queries, pulls, deltas, lses = [], [], [], []
         for h in range(heads):
             cut = slice(h * HD, (h + 1) * HD)
-            queries.append(jnp.concatenate([q_all[:, cut] * bf16(SCALE), blank], axis=1))
-            pulls.append(jnp.concatenate([blank, d_all[:, cut]], axis=1))
-            deltas.append(jnp.sum(both[:, cut], axis=1, keepdims=True))
-            lses.append(lse_ref[h, rows, :])
-        stacks = [jnp.concatenate([queries[h], pulls[h]], axis=0) for h in range(heads)]
-        first, last = tile_span(span_ref, tile, step * block, block)
-
-        def body(kt, state):
-            cols = pl.ds(pl.multiple_of(kt * KT, KT), KT)
-            same = qid == kid_ref[0, :, cols]
-            out = []
+            stack_ref[h, :QT, :] = jnp.concatenate([q_all[:, cut] * bf16(SCALE), blank], axis=1)
+            stack_ref[h, QT:, :] = jnp.concatenate([blank, d_all[:, cut]], axis=1)
+            delta_ref[h] = spread(jnp.sum(both[:, cut], axis=1, keepdims=True))
+        start, count = tile_span(span_ref, tile, step * block, block)
+
+        def body(i, _):
+            cols = pl.ds(pl.multiple_of(start + i * KT, 128), KT)
+            same = twice(qid_ref[rows, :]) == kid_ref[0, :, cols]
             for h in range(heads):
-                kv = kv_ref[cols, h * 128 : (h + 1) * 128]
-                s = jnp.where(same, dot(queries[h], kv, NT), MASKED)
-                p = jnp.exp(s - lses[h])
-                dp = dot(pulls[h], kv, NT)
-                ds = (p * (dp - deltas[h])).astype(bf16)
-                out.append(state[h] + dot(ds, kv))
+                lanes = slice(h * 128, (h + 1) * 128)
+                kv = kv_ref[cols, lanes]
+                s = jnp.where(same, dot(stack_ref[h, :QT, :], kv, NT), MASKED)
+                p = jnp.exp(s - twice(lse_ref[h, rows, :]))
+                dp = dot(stack_ref[h, QT:, :], kv, NT)
+                ds = (p * (dp - twice(delta_ref[h]))).astype(bf16)
+                dq_acc[h, rows, :] += dot(ds, kv)
                 pair = jnp.concatenate([ds, p.astype(bf16)], axis=0)
-                dkv_acc[cols, h * 128 : (h + 1) * 128] += dot(pair, stacks[h], TN)
-            return tuple(out)
-
-        state = tuple(dq_acc[h, rows, :] for h in range(heads))
-        state = lax.fori_loop(first, last, body, state)
-        for h in range(heads):
-            dq_acc[h, rows, :] = state[h]
+                dkv_acc[cols, lanes] += dot(pair, stack_ref[h], TN)
+            return 0
+
+        lax.fori_loop(0, count, body, 0)
 
         @pl.when(step == steps - 1)
         def _():
             dq_ref[rows, :] = jnp.concatenate(
-                [state[h][:, :HD] * SCALE for h in range(heads)], axis=1
+                [dq_acc[h, rows, :HD] * SCALE for h in range(heads)], axis=1
             ).astype(bf16)
 
         return 0
@@ -206,7 +217,7 @@
                 pl.BlockSpec((block, kv.shape[1]), lambda s, _: (s, 0)),
                 pl.BlockSpec(q.shape, whole),
                 pl.BlockSpec(q.shape, whole),
-                pl.BlockSpec((heads, rows, 1), lambda s, _: (0, 0, 0)),
+                pl.BlockSpec((heads, rows, 128), lambda s, _: (0, 0, 0)),
             ],
             out_specs=[
                 pl.BlockSpec(q.shape, whole),
@@ -215,6 +226,8 @@
             scratch_shapes=[
                 pltpu.VMEM((heads, rows, 128), f32),
                 pltpu.VMEM((block, kv.shape[1]), f32),
+                pltpu.VMEM((heads, QT, 128), f32),
+                pltpu.VMEM((heads, 2 * QT, 128), bf16),
             ],
         ),
         out_shape=[
@@ -258,27 +271,26 @@
     my_mp = lax.axis_index("mp")
     flip = (my_mp // 2) % 2 == 1
 
+    wide = 3 * head_cols
+    kv_cols = 2 * head_cols
     kv_shard = jnp.stack(
         [w_qkv[:, 1].reshape(band, heads, HD), w_qkv[:, 2].reshape(band, heads, HD)], axis=2
-    ).reshape(band, 2 * head_cols)
-    qkv_shard = jnp.concatenate([w_qkv[:, 0], kv_shard], axis=1)
+    ).reshape(band, kv_cols)
+    shard_one = jnp.concatenate([kv_shard, w_qkv[:, 0]], axis=1)
+    got_one = lax.all_gather(shard_one, OWNER, axis=0, tiled=True)
     smalls = (b_qv, b_up, gains, biases)
-    small_sizes = [s.size for s in smalls]
-    line = jnp.concatenate([s.reshape(-1) for s in smalls])
-    wide = 3 * head_cols
-    tall = (band + 1 + 15) // 16 * 16
-    line = jnp.pad(line, (0, wide - line.shape[0]))[None]
-    shard_one = jnp.concatenate([qkv_shard, jnp.pad(line, ((0, tall - band - 1), (0, 0)))], axis=0)
-    got_one = lax.all_gather(shard_one, OWNER, axis=0, tiled=True).reshape(mp, dp, tall, wide)
+    small_sizes = [a.size for a in smalls]
+    line = jnp.concatenate([a.reshape(-1) for a in smalls])
+    line = jnp.pad(line, (0, 1024 - line.shape[0])).reshape(1, 8, 128)
+    lines = lax.all_to_all(jnp.broadcast_to(line, (mp * dp, 8, 128)), OWNER, 0, 0, tiled=True)
     x_bf = lax.all_to_all(frames, "mb", 0, 0, tiled=True).reshape(rows, width)
+    g_bf = lax.all_to_all(cotangent, "mb", 0, 0, tiled=True).reshape(rows, width)
     shard_two = jnp.concatenate([w_up, w_down.T, w_out.T], axis=1)
-    shard_two = lax.optimization_barrier((shard_two, got_one))
-    got_one = shard_two[1]
-    got_two = lax.all_gather(shard_two[0], OWNER, axis=0, tiled=True).reshape(mp, width, 2 * ff + head_cols)
-    g_bf = lax.all_to_all(cotangent, "mb", 0, 0, tiled=True).reshape(rows, width)
-
-    weight_qkv = got_one[:, :, :band].reshape(mp, width, wide)
-    lines = got_one[:, :, band].astype(f32)
+    shard_two, x_bf, g_bf, lines = lax.optimization_barrier((shard_two, x_bf, g_bf, lines))
+    got_two = lax.all_gather(shard_two, OWNER, axis=0, tiled=True).reshape(mp, width, 2 * ff + head_cols)
+
+    weight_qkv = got_one.reshape(mp, width, wide)
+    lines = lines.reshape(mp, dp, 1024).astype(f32)
     cuts = []
     at = 0
     for size in small_sizes:
@@ -313,7 +325,7 @@
         ]
     )
     block = min(seq, 4608)
-    qid = qid[:, None]
+    qid = jnp.broadcast_to(qid[:, None], (qid.shape[0], 128))
     kid = clip_row.reshape(seq // block, 1, block)
 
     def to_parts(q):
@@ -348,10 +360,10 @@
     bias_q = bias_qv[0]
     bias_v = bias_qv[1].reshape(mp, heads, 1, HD)
     bias_kv = jnp.concatenate([jnp.zeros_like(bias_v), bias_v], axis=2).reshape(mp, 2 * head_cols)
-    bias_all = jnp.concatenate([bias_q, bias_kv], axis=1)
+    bias_all = jnp.concatenate([bias_kv, bias_q], axis=1)
     proj = jnp.stack([(dot(h1, weight_qkv[m]) + bias_all[m]).astype(bf16) for m in range(mp)])
-    kv_part = jnp.broadcast_to(proj[None, :, :, head_cols:], (parts, mp, rows, 2 * head_cols))
-    sent = jnp.concatenate([to_parts(proj[:, :, :head_cols]), kv_part], axis=2)
+    kv_part = jnp.broadcast_to(proj[None, :, :, :kv_cols], (parts, mp, rows, 2 * head_cols))
+    sent = jnp.concatenate([to_parts(proj[:, :, kv_cols:]), kv_part], axis=2)
     came = swap(sent)
     q_tiles = to_tiles(came[:, :, :half])
     kv_seq = (
@@ -386,6 +398,7 @@
     datt_tiles = to_tiles(swap(to_parts(datt)))
     outs = [dot(drb, att[m], TN).astype(bf16) for m in range(mp)]
     grads_two = jnp.stack([jnp.concatenate([ups[m], downs[m], outs[m]], axis=1) for m in range(mp)])
+    datt_tiles, grads_two = lax.optimization_barrier((datt_tiles, grads_two))
     mine_two = lax.psum_scatter(
         grads_two.reshape(mp * width, 2 * ff + head_cols), OWNER, scatter_dimension=0, tiled=True
     ).astype(f32)
@@ -395,7 +408,7 @@
     back = swap(jnp.concatenate([from_tiles(dq_tiles), dkv], axis=2))
     dq = from_parts(back[:, :, :half])
     dkv = jnp.sum(back[:, :, half:], axis=0, dtype=f32).astype(bf16)
-    dproj = jnp.concatenate([dq, dkv], axis=2)
+    dproj = jnp.concatenate([dkv, dq], axis=2)
     grad_one = jnp.zeros((rows, width), f32)
     for m in range(mp):
         grad_one = grad_one + dot(dproj[m], weight_qkv[m], NT)
@@ -403,9 +416,12 @@
     frames_grad = lax.all_to_all(dx.reshape(mbs, share, width), "mb", 0, 0, tiled=True)
 
     grads_qkv = jnp.stack([dot(h1, dproj[m], TN).astype(bf16) for m in range(mp)])
+    spans = grads_qkv.reshape(mp, mbs, parts, band, wide).transpose(2, 0, 1, 3, 4)
+    plane_sum = jnp.sum(swap(spans).reshape(parts * mp, mbs, band, wide), axis=0, dtype=f32).astype(bf16)
+    mine_one = jnp.sum(lax.all_to_all(plane_sum, "mb", 0, 0, tiled=True), axis=0, dtype=f32)
     col_sums = jnp.sum(dproj, axis=1, dtype=f32)
-    dbq = col_sums[:, :head_cols].reshape(mp, dp, 1, -1)
-    dbv = col_sums[:, head_cols:].reshape(mp, heads, 2, HD)[:, :, 1].reshape(mp, dp, 1, -1)
+    dbq = col_sums[:, kv_cols:].reshape(mp, dp, 1, -1)
+    dbv = col_sums[:, :kv_cols].reshape(mp, heads, 2, HD)[:, :, 1].reshape(mp, dp, 1, -1)
     dbup = jnp.stack(bups).reshape(mp, dp, -1)
     dgains = jnp.stack([jnp.sum(grad_one * hat_one, axis=0), jnp.sum(grad_two * hat_two, axis=0)])
     dbiases = jnp.stack(
@@ -418,23 +434,18 @@
     small = jnp.concatenate(
         [jnp.concatenate([dbq, dbv], axis=2).reshape(mp, dp, -1), dbup, by_owner(dgains), by_owner(dbiases)], axis=2
     )
-    small = jnp.pad(small, ((0, 0), (0, 0), (0, wide - small.shape[2])))[:, :, None].astype(bf16)
-    small = jnp.pad(small, ((0, 0), (0, 0), (0, tall - band - 1), (0, 0)))
-    grads_one = jnp.concatenate([grads_qkv.reshape(mp, dp, band, wide), small], axis=2)
-    mine_one = lax.psum_scatter(
-        grads_one.reshape(mp * dp * tall, wide), OWNER, scatter_dimension=0, tiled=True
-    ).astype(f32)
-
-    kv_mine = mine_one[:band, head_cols:].reshape(band, heads, 2, HD)
+    small = jnp.pad(small, ((0, 0), (0, 0), (0, 1024 - small.shape[2]))).reshape(mp * dp, 8, 128)
+    small_mine = jnp.sum(lax.all_to_all(small, OWNER, 0, 0, tiled=True), axis=0).reshape(-1)
+
+    kv_mine = mine_one[:, :kv_cols].reshape(band, heads, 2, HD)
     grad_qkv = jnp.stack(
         [
-            mine_one[:band, :head_cols],
+            mine_one[:, kv_cols:],
             kv_mine[:, :, 0].reshape(band, head_cols),
             kv_mine[:, :, 1].reshape(band, head_cols),
         ],
         axis=1,
     )
-    small_mine = mine_one[band]
     pieces = []
     at = 0
     for size, like in zip(small_sizes, smalls):

time: 998 us -> 755 us (0.76)
  waiting for transfers between devices: 401 us -> 244 us
  local copies, waits for them, and re-layouts: 155 us -> 98.3 us
  Pallas kernels: 158 us -> 107 us
  matrix products: 95.2 us -> 137 us
  starting transfers between devices: 69.1 us -> 55.9 us
    reduce_scatter x1, waiting for transfers between devices: 142 us -> 0.01 us  [local(): lax.psum_scatter(grads_two.reshape(mp * width, 2 * ff + head_cols), OWNER...]
    all_to_all x3 -> x5, waiting for transfers between devices: 97.8 us -> 176 us  [swap(): lax.all_to_all(a.reshape((parts * mp,) + a.shape[2:]), PLANE, 0, 0, tiled...]
    all_gather x2, waiting for transfers between devices: 65 us -> 0.04 us  [the longest x1 0.02 us: local(): got_one = lax.all_gather(shard_one, OWNER, axis=0, tiled=True)]
    pallas_call x1, Pallas kernels: 90.3 us -> 40 us  [attend(): pl.pallas_call(functools.partial(attend_kernel, heads=heads, block=block)...]
    unnamed x5 -> x3, waiting for transfers between devices: 43.7 us -> 0.05 us
    dot_general x48, matrix products: 95.2 us -> 137 us  [dot(): return lax.dot_general(a, b, dims, preferred_element_type=f32)]
    all_to_all x1, waiting for transfers between devices: 0.01 us -> 30.1 us  [local(): lax.all_to_all(cotangent, 'mb', 0, 0, tiled=True).reshape(rows, width)]
    all_to_all x1, waiting for transfers between devices: 22.9 us -> 0.01 us  [local(): lax.all_to_all(result.astype(bf16).reshape(mbs, share, width), 'mb', 0, 0...]
  transfers between devices with their start and end apart: 10 -> 13, of which waited for: 8 -> 8; matrix products, arithmetic and copies ran while one was open for 17% -> 16% of each run, Pallas kernels for 9% -> 5%
where the time goes in v2:
time: 755 us; the launch traced here: 745 us
  waiting for transfers between devices  244 us (32%)
  matrix products  137 us (18%)
  Pallas kernels  107 us (14%)
  local copies, waits for them, and re-layouts  98.3 us (13%)
  starting transfers between devices  55.9 us (7%)
  blocking collectives  45.5 us (6%)
  other arithmetic  41.8 us (6%)
  between operations  15.6 us (2%)
    all_to_all x5, waiting for transfers between devices, swap(): lax.all_to_all(a.reshape((parts * mp,) + a.shape[2:]), PLANE, 0, 0, tiled...  176 us
    dot_general x48, matrix products, dot(): return lax.dot_general(a, b, dims, preferred_element_type=f32)  137 us
    pallas_call x1, Pallas kernels, attend_pull(): pl.pallas_call(functools.partial(pull_kernel, heads=heads, block=block),...  67.3 us
    pallas_call x1, Pallas kernels, attend(): pl.pallas_call(functools.partial(attend_kernel, heads=heads, block=block)...  40 us
    all_to_all x1, blocking collectives, local(): x_bf = lax.all_to_all(frames, 'mb', 0, 0, tiled=True).reshape(rows, width)  31 us
    all_to_all x1, waiting for transfers between devices, local(): lax.all_to_all(cotangent, 'mb', 0, 0, tiled=True).reshape(rows, width)  30.1 us
    all_to_all x1, waiting for transfers between devices, local(): lax.all_to_all(dx.reshape(mbs, share, width), 'mb', 0, 0, tiled=True)  23.1 us
    all_to_all x5, starting transfers between devices, swap(): lax.all_to_all(a.reshape((parts * mp,) + a.shape[2:]), PLANE, 0, 0, tiled...  21.6 us
  transfers between devices with their start and end apart: 13, of which 8 were waited for; matrix products, arithmetic and copies ran while one was open for 16% of the time, Pallas kernels for 5%

profile of v2, /device:TPU:0, one launch (start us, length us, event | category | flops | bytes accessed | tf_op | source)
XLA Modules:
  0.0 745.2 jit_solution(11116119102159126701)
XLA Ops:
  12.4 14.5 %all_to_all.60 = bf16[32,8,128]{2,1,0:T(8,128)(2,1)S(1)} all-to-all(bf16[32,8,128]{2,1,0:T(8,128)(2,1)S(1)} %broadcast_in_dim.19), channel_id=1, replica_groups=mesh['mb'=4,'part'=2,'mp'=4] {'mp','mb','part'}, dimensions={0} | all-to-all | bytes 131072 | tf_op jit(solution)/shard_map/all_to_all | solution.py:285
  26.9 31.0 %all_to_all.61 = bf16[4,144,768]{2,1,0:T(8,128)(2,1)S(1)} all-to-all(bf16[4,144,768]{2,1,0:T(8,128)(2,1)S(1)} %copy-done.34), channel_id=1, replica_groups=mesh['mb'=4,'part'=2,'mp'=4] {'mb'}, dimensions={0} | all-to-all | bytes 1769472 | tf_op jit(solution)/shard_map/all_to_all | solution.py:286
  62.4 30.1 %all-to-all-done.1 = bf16[4,144,768]{2,1,0:T(8,128)(2,1)S(1)} async-done(((bf16[4,144,768]{2,1,0:T(8,128)(2,1)}), bf16[4,144,768]{2,1,0:T(8,128)(2,1)S(1)}, u32[]{:S(2)}, u32[]{:S(2)}) %all-to-all-start.1) | async-done | bytes 884768 | tf_op jit(solution)/shard_map/all_to_all | solution.py:287
  108.7 4.8 all-to-all-start.3
  117.0 75.8 %all-to-all-done.3 = bf16[8,720,384]{2,1,0:T(8,128)(2,1)} async-done(((bf16[8,720,384]{2,1,0:T(8,128)(2,1)}), bf16[8,720,384]{2,1,0:T(8,128)(2,1)}, u32[]{:S(2)}, u32[]{:S(2)}) %all-to-all-start.3) | async-done | bytes 4423712 | tf_op jit(solution)/shard_map/all_to_all | solution.py:355
  194.1 4.4 slice.357
  206.6 40.0 %attend.1 = (bf16[2304,192]{1,0:T(8,128)(2,1)}, f32[3,2304,128]{2,1,0:T(8,128)}) custom-call(s32[2,8]{1,0:T(2,128)} %pad_add_fusion.span_ref, bf16[2304,192]{1,0:T(8,128)(2,1)} %bitcast.291, s32[2304,128]{1,0:T(8,128)} %broadcast_in_dim.23.qid_ref, s32[1,1,4608]{2,1,0:T(1,128)} %get-tuple-element.124.kid_ref, bf16[4608,384]{1,0:T(8,128)(2,1)} %bitcast.285), custom_call_target="tpu_custom_call" | custom-call | tf_op jit(solution)/shard_map/attend/pallas_call | solution.py:122
  255.2 12.9 %all-to-all-done.4 = bf16[8,144,384]{2,1,0:T(8,128)(2,1)S(1)} async-done(((bf16[8,144,384]{2,1,0:T(8,128)(2,1)}), bf16[8,144,384]{2,1,0:T(8,128)(2,1)S(1)}, u32[]{:S(2)}, u32[]{:S(2)}) %all-to-all-start.4) | async-done | bytes 884768 | tf_op jit(solution)/shard_map/all_to_all | solution.py:355
  278.3 12.1 %multiply_convert_fusion.1 = (bf16[576,768]{1,0:T(8,128)(2,1)}, f32[576,768]{1,0:T(8,128)S(1)}, f32[576,768]{1,0:T(8,128)S(1)}) fusion(f32[768]{0:T(1024)S(1)} %add.269, bf16[576,768]{1,0:T(8,128)(2,1)S(1)} %add_convert_fusion.5, bf16[4,768,1728]{2,1,0:T(8,128)(2,1)S(1)} %bitcast.326), kind=kOutput, calls=%fused_computation.84 | convolution fusion | flops 708673536 | bytes 6492160 | tf_op jit(solution)/shard_map/dot_general | solution.py:27
  290.4 12.1 %multiply_convert_fusion.2 = (bf16[576,768]{1,0:T(8,128)(2,1)}, f32[576,768]{1,0:T(8,128)S(1)}, f32[576,768]{1,0:T(8,128)S(1)}) fusion(f32[768]{0:T(1024)S(1)} %add.265, bf16[576,768]{1,0:T(8,128)(2,1)S(1)} %add_convert_fusion.5, bf16[4,768,1728]{2,1,0:T(8,128)(2,1)S(1)} %bitcast.327), kind=kOutput, calls=%fused_computation.97 | convolution fusion | flops 708673536 | bytes 6492160 | tf_op jit(solution)/shard_map/dot_general | solution.py:27
  302.5 24.4 %multiply_convert_fusion.3 = (bf16[576,768]{1,0:T(8,128)(2,1)}, f32[576,768]{1,0:T(8,128)S(1)}, f32[576,768]{1,0:T(8,128)S(1)}) fusion(f32[768]{0:T(1024)S(1)} %add.261, bf16[576,768]{1,0:T(8,128)(2,1)S(1)} %add_convert_fusion.5, bf16[4,768,1728]{2,1,0:T(8,128)(2,1)S(1)} %bitcast.328), kind=kOutput, calls=%fused_computation.110 | convolution fusion | flops 708673536 | bytes 6492160 | tf_op jit(solution)/shard_map/dot_general | solution.py:27
  326.9 12.1 %multiply_convert_fusion = (bf16[576,768]{1,0:T(8,128)(2,1)}, f32[576,768]{1,0:T(8,128)S(1)}, f32[576,768]{1,0:T(8,128)S(1)}) fusion(f32[768]{0:T(1024)S(1)} %add.273, bf16[576,768]{1,0:T(8,128)(2,1)S(1)} %add_convert_fusion.5, bf16[4,768,1728]{2,1,0:T(8,128)(2,1)S(1)} %bitcast.329), kind=kOutput, calls=%fused_computation.71 | convolution fusion | flops 708673536 | bytes 6492160 | tf_op jit(solution)/shard_map/dot_general | solution.py:27
  398.6 5.3 pad_maximum_fusion
  407.9 67.3 %attend_pull.1 = (bf16[2304,192]{1,0:T(8,128)(2,1)}, bf16[4608,384]{1,0:T(8,128)(2,1)}) custom-call(s32[2,8]{1,0:T(2,128)} %pad_add_fusion.span_ref, bf16[2304,192]{1,0:T(8,128)(2,1)} %bitcast.292, s32[2304,128]{1,0:T(8,128)} %broadcast_in_dim.23.qid_ref, s32[1,1,4608]{2,1,0:T(1,128)} %get-tuple-element.124.kid_ref, bf16[4608,384]{1,0:T(8,128)(2,1)} %bitcast.286, ...), custom_call_target="tpu_custom_call" | custom-call | tf_op jit(solution)/shard_map/attend_pull/pallas_call | solution.py:208
  484.8 13.8 %copy.202 = bf16[4,768,1728]{2,1,0:T(8,128)(2,1)} copy(bf16[4,768,1728]{1,2,0:T(8,128)(2,1)} %pad_maximum_fusion) | data formatting | bytes 21233664 | tf_op jit(solution)/shard_map/optimization_barrier | solution.py:401
  498.6 4.6 pad_maximum_fusion.3
  503.2 4.6 all-to-all-start.7
  519.1 40.3 %all-to-all-done.7 = bf16[8,720,384]{2,1,0:T(8,128)(2,1)} async-done(((bf16[8,720,384]{2,1,0:T(8,128)(2,1)}), bf16[8,720,384]{2,1,0:T(8,128)(2,1)}, u32[]{:S(2)}, u32[]{:S(2)}) %all-to-all-start.7) | async-done | bytes 4423712 | tf_op jit(solution)/shard_map/all_to_all | solution.py:355
  559.4 18.2 %all-to-all-start.5 = ((bf16[4,144,768]{2,1,0:T(8,128)(2,1)}), bf16[4,144,768]{2,1,0:T(8,128)(2,1)}, u32[]{:S(2)}, u32[]{:S(2)}) async-start(bf16[4,144,768]{2,1,0:T(8,128)(2,1)} %bitcast.51), calls=%async_computation.5 | async-start | bytes 1769472 | tf_op jit(solution)/shard_map/all_to_all | solution.py:393
  626.9 4.8 all-to-all-start.9
  634.7 47.1 %all-to-all-done.9 = bf16[8,4,96,576]{3,2,1,0:T(8,128)(2,1)} async-done(((bf16[8,4,96,576]{3,2,1,0:T(8,128)(2,1)}), bf16[8,4,96,576]{3,2,1,0:T(8,128)(2,1)}, u32[]{:S(2)}, u32[]{:S(2)}) %all-to-all-start.9) | async-done | bytes 3538976 | tf_op jit(solution)/shard_map/all_to_all | solution.py:355
  681.8 4.6 all-to-all-start.8
  690.0 23.1 %all-to-all-done.8 = bf16[4,144,768]{2,1,0:T(8,128)(2,1)S(1)} async-done(((bf16[4,144,768]{2,1,0:T(8,128)(2,1)}), bf16[4,144,768]{2,1,0:T(8,128)(2,1)S(1)}, u32[]{:S(2)}, u32[]{:S(2)}) %all-to-all-start.8) | async-done | bytes 884768 | tf_op jit(solution)/shard_map/all_to_all | solution.py:416
  719.2 11.4 %all-to-all-done.10 = bf16[4,96,576]{2,1,0:T(8,128)(2,1)S(1)} async-done(((bf16[4,96,576]{2,1,0:T(8,128)(2,1)}), bf16[4,96,576]{2,1,0:T(8,128)(2,1)S(1)}, u32[]{:S(2)}, u32[]{:S(2)}) %all-to-all-start.10) | async-done | bytes 442400 | tf_op jit(solution)/shard_map/all_to_all | solution.py:421
  (369 shorter events, 210.2 us)
Async XLA Ops:
  7.2 19.7 %copy-start.34 = (bf16[4,144,768]{2,1,0:T(8,128)(2,1)S(1)}, bf16[4,144,768]{2,1,0:T(8,128)(2,1)}, u32[]{:S(2)}) copy-start(bf16[4,144,768]{2,1,0:T(8,128)(2,1)} %param.11) | copy-start | bytes 2654212
  7.2 87.8 %all-gather.3.cloned.1.call-start = ((), (), s32[]{:S(2)}) async-start(), calls=%async_computation.13 | async-start | bytes 4055040 | tf_op jit(solution)/shard_map/all_gather | solution.py:280
  26.9 34.6 %copy-start.40 = (bf16[192,96]{1,0:T(8,128)(2,1)S(1)}, bf16[192,96]{1,0:T(8,128)(2,1)}, u32[]{:S(2)}) copy-start(bf16[192,96]{1,0:T(8,128)(2,1)} %param.15) | copy-start | bytes 110596
  26.9 34.7 %copy-start.35 = (bf16[768,96]{0,1:T(8,128)(2,1)S(1)}, bf16[768,96]{0,1:T(8,128)(2,1)}, u32[]{:S(2)}) copy-start(bf16[768,96]{0,1:T(8,128)(2,1)} %param.18) | copy-start | bytes 442372
  26.9 34.7 %copy-start.36 = (bf16[96,768]{1,0:T(8,128)(2,1)S(1)}, bf16[96,768]{1,0:T(8,128)(2,1)}, u32[]{:S(2)}) copy-start(bf16[96,768]{1,0:T(8,128)(2,1)} %param.16) | copy-start | bytes 442372
  57.9 217.6 %copy-start = (bf16[4,144,768]{2,1,0:T(8,128)(2,1)}, bf16[4,144,768]{2,1,0:T(8,128)(2,1)S(1)}, u32[]{:S(2)}) copy-start(bf16[4,144,768]{2,1,0:T(8,128)(2,1)S(1)} %all_to_all.61) | copy-start | bytes 2654212
  57.9 34.6 %all-to-all-start.1 = ((bf16[4,144,768]{2,1,0:T(8,128)(2,1)}), bf16[4,144,768]{2,1,0:T(8,128)(2,1)S(1)}, u32[]{:S(2)}, u32[]{:S(2)}) async-start(bf16[4,144,768]{2,1,0:T(8,128)(2,1)} %param.21), calls=%async_computation.1 | async-start | bytes 1769472 | tf_op jit(solution)/shard_map/all_to_all | solution.py:287
  61.4 209.3 %all-gather.5.cloned.1.call-start = ((), (), s32[]{:S(2)}) async-start(), calls=%async_computation.14 | async-start | bytes 11354112 | tf_op jit(solution)/shard_map/all_gather | solution.py:290
  94.0 5.5 copy-start.47
  108.7 84.1 %all-to-all-start.3 = ((bf16[8,720,384]{2,1,0:T(8,128)(2,1)}), bf16[8,720,384]{2,1,0:T(8,128)(2,1)}, u32[]{:S(2)}, u32[]{:S(2)}) async-start(bf16[8,720,384]{2,1,0:T(8,128)(2,1)} %pad_maximum_fusion.2), calls=%async_computation.3 | async-start | bytes 8847360 | tf_op jit(solution)/shard_map/all_to_all | solution.py:355
  250.6 17.4 %all-to-all-start.4 = ((bf16[8,144,384]{2,1,0:T(8,128)(2,1)}), bf16[8,144,384]{2,1,0:T(8,128)(2,1)S(1)}, u32[]{:S(2)}, u32[]{:S(2)}) async-start(bf16[8,144,384]{2,1,0:T(8,128)(2,1)} %reshape_reshape.17), calls=%async_computation.4 | async-start | bytes 1769472 | tf_op jit(solution)/shard_map/all_to_all | solution.py:355
  255.1 47.4 %copy-start.53 = (f32[768]{0:T(1024)}, f32[768]{0:T(1024)S(1)}, u32[]{:S(2)}) copy-start(f32[768]{0:T(1024)S(1)} %add.261) | copy-start | bytes 9220
  270.8 7.5 %slice-start = ((s8[11010048]{0:T(1024)(128)(4,1)}), s8[4194304]{0:T(1024)(128)(4,1)S(1)}, s32[]{:S(2)}) async-start(s8[11010048]{0:T(1024)(128)(4,1)} %bitcast.324), calls=%async_computation.16 | async-start | bytes 8388608
  326.9 12.1 %copy-start.10 = (bf16[4,144,768]{2,1,0:T(8,128)(2,1)S(1)}, bf16[4,144,768]{2,1,0:T(8,128)(2,1)}, u32[]{:S(2)}) copy-start(bf16[4,144,768]{2,1,0:T(8,128)(2,1)} %copy-done.9) | copy-start | bytes 2654212
  384.8 19.1 %all-to-all-start.6 = ((bf16[8,144,384]{2,1,0:T(8,128)(2,1)}), bf16[8,144,384]{2,1,0:T(8,128)(2,1)S(1)}, u32[]{:S(2)}, u32[]{:S(2)}) async-start(bf16[8,144,384]{2,1,0:T(8,128)(2,1)} %reshape_reshape.19), calls=%async_computation.6 | async-start | bytes 1769472 | tf_op jit(solution)/shard_map/all_to_all | solution.py:355
  388.4 343.4 %reduce-scatter.2.cloned.1.call-start = ((), (), s32[]{:S(2)}) async-start(), calls=%async_computation.15 | async-start | bytes 11354112 | tf_op jit(solution)/shard_map/reduce_scatter | solution.py:402
  503.2 5.4 copy-start.50
  503.2 56.2 %all-to-all-start.7 = ((bf16[8,720,384]{2,1,0:T(8,128)(2,1)}), bf16[8,720,384]{2,1,0:T(8,128)(2,1)}, u32[]{:S(2)}, u32[]{:S(2)}) async-start(bf16[8,720,384]{2,1,0:T(8,128)(2,1)} %pad_maximum_fusion.3), calls=%async_computation.7 | async-start | bytes 8847360 | tf_op jit(solution)/shard_map/all_to_all | solution.py:355
  559.4 55.2 %all-to-all-start.5 = ((bf16[4,144,768]{2,1,0:T(8,128)(2,1)}), bf16[4,144,768]{2,1,0:T(8,128)(2,1)}, u32[]{:S(2)}, u32[]{:S(2)}) async-start(bf16[4,144,768]{2,1,0:T(8,128)(2,1)} %bitcast.51), calls=%async_computation.5 | async-start | bytes 1769472 | tf_op jit(solution)/shard_map/all_to_all | solution.py:393
  612.9 6.1 copy-start.6
  614.7 12.2 %all-to-all-start.11 = ((f32[32,8,128]{2,1,0:T(8,128)}), f32[32,8,128]{2,1,0:T(8,128)S(1)}, u32[]{:S(2)}, u32[]{:S(2)}) async-start(f32[32,8,128]{2,1,0:T(8,128)} %bitcast.104), calls=%async_computation.11 | async-start | bytes 262144 | tf_op jit(solution)/shard_map/all_to_all | solution.py:438
  626.9 54.9 %all-to-all-start.9 = ((bf16[8,4,96,576]{3,2,1,0:T(8,128)(2,1)}), bf16[8,4,96,576]{3,2,1,0:T(8,128)(2,1)}, u32[]{:S(2)}, u32[]{:S(2)}) async-start(bf16[8,4,96,576]{3,2,1,0:T(8,128)(2,1)} %bitcast.287), calls=%async_computation.9 | async-start | bytes 7864320 | tf_op jit(solution)/shard_map/all_to_all | solution.py:355
  681.8 31.3 %all-to-all-start.8 = ((bf16[4,144,768]{2,1,0:T(8,128)(2,1)}), bf16[4,144,768]{2,1,0:T(8,128)(2,1)S(1)}, u32[]{:S(2)}, u32[]{:S(2)}) async-start(bf16[4,144,768]{2,1,0:T(8,128)(2,1)} %bitcast.75), calls=%async_computation.8 | async-start | bytes 1769472 | tf_op jit(solution)/shard_map/all_to_all | solution.py:416
  713.1 17.5 %all-to-all-start.10 = ((bf16[4,96,576]{2,1,0:T(8,128)(2,1)}), bf16[4,96,576]{2,1,0:T(8,128)(2,1)S(1)}, u32[]{:S(2)}, u32[]{:S(2)}) async-start(bf16[4,96,576]{2,1,0:T(8,128)(2,1)} %reduce_sum.242), calls=%async_computation.10 | async-start | bytes 983040 | tf_op jit(solution)/shard_map/all_to_all | solution.py:421
  (54 other events, 143.3 us)
Sparse Core Ops, SparseCore 0:
  11.5 72.6 all-gather.2
  92.6 113.0 all-gather.4
  498.8 203.8 reduce-scatter.1

commit v3 on v2

--- a/solution.py
+++ b/solution.py
@@ -238,6 +238,89 @@
     )(span, q, qid, kid, kv, datt, att, lse)
 
 
+def feed_kernel(h2_ref, g_ref, w_ref, b_ref, res_ref, two_ref, grad_ref, bup_ref, act_ref, du_ref, *, ff):
+    @pl.when(pl.program_id(0) == 0)
+    def _():
+        res_ref[...] = jnp.zeros(res_ref.shape, f32)
+        two_ref[...] = jnp.zeros(two_ref.shape, f32)
+
+    def chunk(i, _):
+        rows = pl.ds(pl.multiple_of(i * QT, QT), QT)
+        u = dot(h2_ref[rows, :], w_ref[0, :, :ff]) + b_ref[0]
+        below = 0.5 + 0.5 * lax.erf(u * 0.7071067811865476)
+        slope = below + u * (jnp.exp(u * u * -0.5) * 0.3989422804014327)
+        act = (u * below).astype(bf16)
+        du = (dot(g_ref[rows, :], w_ref[0, :, ff : 2 * ff]) * slope).astype(bf16)
+        act_ref[rows, :] = act
+        du_ref[rows, :] = du
+        res_ref[rows, :] += dot(act, w_ref[0, :, ff : 2 * ff], NT)
+        two_ref[rows, :] += dot(du, w_ref[0, :, :ff], NT)
+        return 0
+
+    lax.fori_loop(0, h2_ref.shape[0] // QT, chunk, 0)
+    grad_ref[0, :, :ff] = dot(h2_ref[...], du_ref[...], TN).astype(bf16)
+    grad_ref[0, :, ff : 2 * ff] = dot(g_ref[...], act_ref[...], TN).astype(bf16)
+    grad_ref[0, :, 2 * ff :] = jnp.zeros((grad_ref.shape[1], grad_ref.shape[2] - 2 * ff), bf16)
+    bup_ref[0] = jnp.sum(du_ref[...].astype(f32), axis=0, keepdims=True)
+
+
+def feed_forward(h2, g, weights, bias, grad_wide):
+    mp, width, w_wide = weights.shape
+    rows = h2.shape[0]
+    ff = bias.shape[2]
+    whole = lambda m: (0, 0)
+    each = lambda m: (m, 0, 0)
+    return pl.pallas_call(
+        functools.partial(feed_kernel, ff=ff),
+        grid=(mp,),
+        in_specs=[
+            pl.BlockSpec(h2.shape, whole),
+            pl.BlockSpec(g.shape, whole),
+            pl.BlockSpec((1, width, w_wide), each),
+            pl.BlockSpec((1, 1, ff), each),
+        ],
+        out_specs=[
+            pl.BlockSpec((rows, width), whole),
+            pl.BlockSpec((rows, width), whole),
+            pl.BlockSpec((1, width, grad_wide), each),
+            pl.BlockSpec((1, 1, ff), each),
+        ],
+        scratch_shapes=[pltpu.VMEM((rows, ff), bf16), pltpu.VMEM((rows, ff), bf16)],
+        out_shape=[
+            jax.ShapeDtypeStruct((rows, width), f32),
+            jax.ShapeDtypeStruct((rows, width), f32),
+            jax.ShapeDtypeStruct((mp, width, grad_wide), bf16),
+            jax.ShapeDtypeStruct((mp, 1, ff), f32),
+        ],
+        name="feed_forward",
+    )(h2, g, weights, bias)
+
+
+def out_kernel(drb_ref, att_ref, _, grad_ref):
+    grad = dot(drb_ref[...], att_ref[0], TN).astype(bf16)
+    rest = grad_ref.shape[2] - grad.shape[1]
+    grad_ref[0] = jnp.concatenate([grad, jnp.zeros((grad.shape[0], rest), bf16)], axis=1)
+
+
+def out_grads(drb, att, grads, place):
+    mp, rows, cols = att.shape
+    width = drb.shape[1]
+    lanes = grads.shape[2] - place
+    return pl.pallas_call(
+        out_kernel,
+        grid=(mp,),
+        in_specs=[
+            pl.BlockSpec(drb.shape, lambda m: (0, 0)),
+            pl.BlockSpec((1, rows, cols), lambda m: (m, 0, 0)),
+            pl.BlockSpec(memory_space=pl.ANY),
+        ],
+        out_specs=pl.BlockSpec((1, width, lanes), lambda m: (m, 0, place // lanes)),
+        out_shape=jax.ShapeDtypeStruct(grads.shape, bf16),
+        input_output_aliases={2: 0},
+        name="out_grads",
+    )(drb, att, grads)
+
+
 def standard(values):
     middle = jnp.mean(values, axis=-1, keepdims=True)
     centred = values - middle
@@ -248,10 +331,6 @@
 def norm_pull(grad, hat, inverse, gain):
     t = grad * gain
     return (t - jnp.mean(t, axis=-1, keepdims=True) - hat * jnp.mean(t * hat, axis=-1, keepdims=True)) * inverse
-
-
-def gelu_exact(values):
-    return jax.nn.gelu(values, approximate=False)
 
 
 def local(frames, clip_ids, w_qkv, b_qv, w_out, w_up, b_up, w_down, gains, biases, cotangent):
@@ -297,11 +376,9 @@
         cuts.append(lines[:, :, at : at + size])
         at += size
     bias_qv = cuts[0].reshape(mp, dp, 2, -1).transpose(2, 0, 1, 3).reshape(2, mp, head_cols)
-    bias_up = cuts[1].reshape(mp, ff)
+    bias_up = cuts[1].reshape(mp, 1, ff)
     gain_rows = cuts[2].reshape(mp, dp, 2, -1).transpose(2, 1, 0, 3).reshape(2, width)
     bias_rows = cuts[3].reshape(mp, dp, 4, -1).transpose(2, 1, 0, 3).reshape(4, width)
-    weight_up = got_two[:, :, :ff]
-    weight_down = got_two[:, :, ff : 2 * ff]
     weight_out = got_two[:, :, 2 * ff :]
 
     clip_row = lax.dynamic_index_in_dim(clip_ids, lax.axis_index("mb"), 0, keepdims=False)
@@ -371,41 +448,33 @@
     )
     att_tiles, lse = attend(span, q_tiles, qid, kid, kv_seq, heads, block)
     att = from_parts(swap(from_tiles(att_tiles)))
+    if parts == 2:
+        h1_late, att = lax.optimization_barrier((h1, att))
+        h1_plane = lax.all_gather(h1_late, PLANE, axis=0, tiled=True)
     mixed = x + bias_rows[1]
     for m in range(mp):
         mixed = mixed + dot(att[m], weight_out[m], NT)
     hat_two, inv_two = standard(mixed)
     h2 = (hat_two * gain_rows[1] + bias_rows[2]).astype(bf16)
     g = g_bf.astype(f32)
-    result = mixed + bias_rows[3]
-    grad_two = jnp.zeros((rows, width), f32)
-    ups, downs, bups = [], [], []
-    for m in range(mp):
-        u = dot(h2, weight_up[m]) + bias_up[m]
-        act, pull = jax.vjp(gelu_exact, u)
-        act = act.astype(bf16)
-        result = result + dot(act, weight_down[m], NT)
-        du = pull(dot(g_bf, weight_down[m]))[0].astype(bf16)
-        grad_two = grad_two + dot(du, weight_up[m], NT)
-        ups.append(dot(h2, du, TN).astype(bf16))
-        downs.append(dot(g_bf, act, TN).astype(bf16))
-        bups.append(jnp.sum(du, axis=0, dtype=f32))
+    grad_wide = (2 * ff + head_cols + 255) // 256 * 256
+    fed, grad_two, grads_two, bups = feed_forward(h2, g_bf, got_two, bias_up, grad_wide)
+    result = mixed + fed + bias_rows[3]
     output = lax.all_to_all(result.astype(bf16).reshape(mbs, share, width), "mb", 0, 0, tiled=True)
 
     dr1 = g + norm_pull(grad_two, hat_two, inv_two, gain_rows[1])
     drb = dr1.astype(bf16)
     datt = jnp.stack([dot(drb, weight_out[m]).astype(bf16) for m in range(mp)])
     datt_tiles = to_tiles(swap(to_parts(datt)))
-    outs = [dot(drb, att[m], TN).astype(bf16) for m in range(mp)]
-    grads_two = jnp.stack([jnp.concatenate([ups[m], downs[m], outs[m]], axis=1) for m in range(mp)])
+    grads_two = out_grads(drb, att, grads_two, 2 * ff)
     datt_tiles, grads_two = lax.optimization_barrier((datt_tiles, grads_two))
     mine_two = lax.psum_scatter(
-        grads_two.reshape(mp * width, 2 * ff + head_cols), OWNER, scatter_dimension=0, tiled=True
+        grads_two.reshape(mp * width, grad_wide), OWNER, scatter_dimension=0, tiled=True
     ).astype(f32)
 
     dq_tiles, dkv_seq = attend_pull(span, q_tiles, qid, kid, kv_seq, datt_tiles, att_tiles, lse, heads, block)
-    dkv = dkv_seq.reshape(mbs, parts, mp, share, 2 * head_cols).transpose(1, 2, 0, 3, 4).reshape(parts, mp, rows, 2 * head_cols)
-    back = swap(jnp.concatenate([from_tiles(dq_tiles), dkv], axis=2))
+    dkv_sent = dkv_seq.reshape(mbs, parts, mp, share, 2 * head_cols).transpose(1, 2, 0, 3, 4).reshape(parts, mp, rows, 2 * head_cols)
+    back = swap(jnp.concatenate([from_tiles(dq_tiles), dkv_sent], axis=2))
     dq = from_parts(back[:, :, :half])
     dkv = jnp.sum(back[:, :, half:], axis=0, dtype=f32).astype(bf16)
     dproj = jnp.concatenate([dkv, dq], axis=2)
@@ -415,14 +484,24 @@
     dx = (dr1 + norm_pull(grad_one, hat_one, inv_one, gain_rows[0])).astype(bf16)
     frames_grad = lax.all_to_all(dx.reshape(mbs, share, width), "mb", 0, 0, tiled=True)
 
-    grads_qkv = jnp.stack([dot(h1, dproj[m], TN).astype(bf16) for m in range(mp)])
-    spans = grads_qkv.reshape(mp, mbs, parts, band, wide).transpose(2, 0, 1, 3, 4)
-    plane_sum = jnp.sum(swap(spans).reshape(parts * mp, mbs, band, wide), axis=0, dtype=f32).astype(bf16)
-    mine_one = jnp.sum(lax.all_to_all(plane_sum, "mb", 0, 0, tiled=True), axis=0, dtype=f32)
+    if parts == 2:
+        spot = (jnp.arange(mp)[None] // 2 + my_part) % 2 == jnp.arange(2)[:, None]
+        own = dq_tiles.reshape(2, parts, mp, 1, share, head_cols).transpose(1, 2, 0, 3, 4, 5)
+        own = jnp.where(spot.T[None, :, None, :, None, None], own, bf16(0)).reshape(parts * mp * rows, head_cols)
+        part_qkv = jnp.concatenate(
+            [dot(h1_plane, dkv_sent.reshape(parts * mp * rows, kv_cols), TN), dot(h1_plane, own, TN)], axis=1
+        )
+        part_qkv = part_qkv.astype(bf16).reshape(dp, band, wide)
+        mine_one = jnp.sum(lax.all_to_all(part_qkv, ("mb", "part"), 0, 0, tiled=True), axis=0, dtype=f32)
+    else:
+        grads_qkv = jnp.stack([dot(h1, dproj[m], TN).astype(bf16) for m in range(mp)])
+        spans = grads_qkv.reshape(mp, mbs, parts, band, wide).transpose(2, 0, 1, 3, 4)
+        plane_sum = jnp.sum(swap(spans).reshape(parts * mp, mbs, band, wide), axis=0, dtype=f32).astype(bf16)
+        mine_one = jnp.sum(lax.all_to_all(plane_sum, "mb", 0, 0, tiled=True), axis=0, dtype=f32)
     col_sums = jnp.sum(dproj, axis=1, dtype=f32)
     dbq = col_sums[:, kv_cols:].reshape(mp, dp, 1, -1)
     dbv = col_sums[:, :kv_cols].reshape(mp, heads, 2, HD)[:, :, 1].reshape(mp, dp, 1, -1)
-    dbup = jnp.stack(bups).reshape(mp, dp, -1)
+    dbup = bups.reshape(mp, dp, -1)
     dgains = jnp.stack([jnp.sum(grad_one * hat_one, axis=0), jnp.sum(grad_two * hat_two, axis=0)])
     dbiases = jnp.stack(
         [jnp.sum(grad_one, axis=0), jnp.sum(dr1, axis=0), jnp.sum(grad_two, axis=0), jnp.sum(g, axis=0)]
@@ -456,7 +535,7 @@
         frames_grad,
         grad_qkv,
         pieces[0],
-        mine_two[:, 2 * ff :].T,
+        mine_two[:, 2 * ff : 2 * ff + head_cols].T,
         mine_two[:, :ff],
         pieces[1],
         mine_two[:, ff : 2 * ff].T,

time: 755 us -> 617 us (0.82)
  matrix products: 137 us -> 39.1 us
  waiting for transfers between devices: 244 us -> 189 us
  Pallas kernels: 107 us -> 134 us
  local copies, waits for them, and re-layouts: 98.3 us -> 79.5 us
  blocking collectives: 45.5 us -> 63.9 us
  starting transfers between devices: 55.9 us -> 45.9 us
    dot_general x48 -> x18, matrix products: 137 us -> 39.1 us  [dot(): return lax.dot_general(a, b, dims, preferred_element_type=f32)]
    all_to_all x5 -> x3, waiting for transfers between devices: 176 us -> 116 us  [swap(): lax.all_to_all(a.reshape((parts * mp,) + a.shape[2:]), PLANE, 0, 0, tiled...]
    pallas_call x0 -> x2, Pallas kernels: none -> 30.1 us  [the longest x1 25.2 us: feed_forward(): pl.pallas_call(functools.partial(feed_kernel, ff=ff), grid=(mp,), in_spec...]
    all_to_all x0 -> x1, blocking collectives: none -> 18.4 us  [swap(): lax.all_to_all(a.reshape((parts * mp,) + a.shape[2:]), PLANE, 0, 0, tiled...]
    optimization_barrier x1 -> x0, local copies, waits for them, and re-layouts: 13.8 us -> none  [local(): datt_tiles, grads_two = lax.optimization_barrier((datt_tiles, grads_two))]
    all_to_all x1, waiting for transfers between devices: 0.01 us -> 10.7 us  [local(): lax.all_to_all(result.astype(bf16).reshape(mbs, share, width), 'mb', 0, 0...]
    dot_general x0 -> x1, local copies, waits for them, and re-layouts: none -> 10.6 us  [dot(): return lax.dot_general(a, b, dims, preferred_element_type=f32)]
    convert_element_type x4 -> x0, local copies, waits for them, and re-layouts: 9.16 us -> none  [local(): dot(h1, dproj[m], TN).astype(bf16)]
  transfers between devices with their start and end apart: 13 -> 12, of which waited for: 8 -> 8; matrix products, arithmetic and copies ran while one was open for 16% -> 25% of each run, Pallas kernels for 5% -> 22%
where the time goes in v3:
time: 617 us; the launch traced here: 609 us
  waiting for transfers between devices  189 us (31%)
  Pallas kernels  134 us (22%)
  local copies, waits for them, and re-layouts  79.5 us (13%)
  blocking collectives  63.9 us (10%)
  starting transfers between devices  45.9 us (7%)
  other arithmetic  42 us (7%)
  matrix products  39.1 us (6%)
  between operations  15.3 us (2%)
    all_to_all x3, waiting for transfers between devices, swap(): lax.all_to_all(a.reshape((parts * mp,) + a.shape[2:]), PLANE, 0, 0, tiled...  116 us
    pallas_call x1, Pallas kernels, attend_pull(): pl.pallas_call(functools.partial(pull_kernel, heads=heads, block=block),...  65.3 us
    dot_general x18, matrix products, dot(): return lax.dot_general(a, b, dims, preferred_element_type=f32)  39.1 us
    pallas_call x1, Pallas kernels, attend(): pl.pallas_call(functools.partial(attend_kernel, heads=heads, block=block)...  38.8 us
    all_to_all x1, blocking collectives, local(): x_bf = lax.all_to_all(frames, 'mb', 0, 0, tiled=True).reshape(rows, width)  31 us
    all_to_all x1, waiting for transfers between devices, local(): lax.all_to_all(cotangent, 'mb', 0, 0, tiled=True).reshape(rows, width)  30 us
    pallas_call x1, Pallas kernels, feed_forward(): pl.pallas_call(functools.partial(feed_kernel, ff=ff), grid=(mp,), in_spec...  25.2 us
    all_to_all x1, blocking collectives, swap(): lax.all_to_all(a.reshape((parts * mp,) + a.shape[2:]), PLANE, 0, 0, tiled...  18.4 us
  transfers between devices with their start and end apart: 12, of which 8 were waited for; matrix products, arithmetic and copies ran while one was open for 25% of the time, Pallas kernels for 22%

profile of v3, /device:TPU:0, one launch (start us, length us, event | category | flops | bytes accessed | tf_op | source)
XLA Modules:
  0.0 609.3 jit_solution(6621707433910922379)
XLA Ops:
  12.4 14.5 %all_to_all.55 = bf16[32,8,128]{2,1,0:T(8,128)(2,1)S(1)} all-to-all(bf16[32,8,128]{2,1,0:T(8,128)(2,1)S(1)} %broadcast_in_dim.34), channel_id=1, replica_groups=mesh['mb'=4,'part'=2,'mp'=4] {'mp','mb','part'}, dimensions={0} | all-to-all | bytes 131072 | tf_op jit(solution)/shard_map/all_to_all | solution.py:364
  26.9 31.0 %all_to_all.56 = bf16[4,144,768]{2,1,0:T(8,128)(2,1)S(1)} all-to-all(bf16[4,144,768]{2,1,0:T(8,128)(2,1)S(1)} %copy-done.19), channel_id=1, replica_groups=mesh['mb'=4,'part'=2,'mp'=4] {'mb'}, dimensions={0} | all-to-all | bytes 1769472 | tf_op jit(solution)/shard_map/all_to_all | solution.py:365
  62.4 30.0 %all-to-all-done.1 = bf16[4,144,768]{2,1,0:T(8,128)(2,1)S(1)} async-done(((bf16[4,144,768]{2,1,0:T(8,128)(2,1)}), bf16[4,144,768]{2,1,0:T(8,128)(2,1)S(1)}, u32[]{:S(2)}, u32[]{:S(2)}) %all-to-all-start.1) | async-done | bytes 884768 | tf_op jit(solution)/shard_map/all_to_all | solution.py:366
  110.1 4.6 all-to-all-start.3
  118.5 76.8 %all-to-all-done.3 = bf16[8,720,384]{2,1,0:T(8,128)(2,1)} async-done(((bf16[8,720,384]{2,1,0:T(8,128)(2,1)}), bf16[8,720,384]{2,1,0:T(8,128)(2,1)}, u32[]{:S(2)}, u32[]{:S(2)}) %all-to-all-start.3) | async-done | bytes 4423712 | tf_op jit(solution)/shard_map/all_to_all | solution.py:432
  208.7 38.8 %attend.1 = (bf16[2304,192]{1,0:T(8,128)(2,1)}, f32[3,2304,128]{2,1,0:T(8,128)}) custom-call(s32[2,8]{1,0:T(2,128)} %pad_add_fusion.span_ref, bf16[2304,192]{1,0:T(8,128)(2,1)} %bitcast.206, s32[2304,128]{1,0:T(8,128)} %broadcast_in_dim.38.qid_ref, s32[1,1,4608]{2,1,0:T(1,128)} %get-tuple-element.123.kid_ref, bf16[4608,384]{1,0:T(8,128)(2,1)} %bitcast.186), custom_call_target="tpu_custom_call" | custom-call | tf_op jit(solution)/shard_map/attend/pallas_call | solution.py:122
  250.6 18.4 %all_to_all.57 = bf16[8,144,384]{2,1,0:T(8,128)(2,1)} all-to-all(bf16[8,144,384]{2,1,0:T(8,128)(2,1)S(1)} %reshape_reshape.20), channel_id=1, replica_groups=mesh['mb'=4,'part'=2,'mp'=4] {'part','mp'}, dimensions={0} | all-to-all | bytes 1769472 | tf_op jit(solution)/shard_map/all_to_all | solution.py:432
  283.3 25.2 %feed_forward.1 = (f32[576,768]{1,0:T(8,128)}, f32[576,768]{1,0:T(8,128)}, bf16[4,768,1792]{2,1,0:T(8,128)(2,1)}, f32[4,1,768]{2,1,0:T(1,128)}) custom-call(bf16[576,768]{1,0:T(8,128)(2,1)} %add_convert_fusion.1.h2_ref, bf16[576,768]{1,0:T(8,128)(2,1)} %bitcast.208, bf16[4,768,1728]{2,1,0:T(8,128)(2,1)} %bitcast.192, f32[4,1,768]{2,1,0:T(1,128)} %reshape.446.b_ref), custom_call_target="tpu_custom_call" | custom-call | tf_op jit(solution)/shard_map/feed_forward/pallas_call | solution.py:273
  330.0 4.9 out_grads.1
  334.9 8.6 %all-to-all-done.6 = bf16[8,144,384]{2,1,0:T(8,128)(2,1)S(1)} async-done(((bf16[8,144,384]{2,1,0:T(8,128)(2,1)}), bf16[8,144,384]{2,1,0:T(8,128)(2,1)S(1)}, u32[]{:S(2)}, u32[]{:S(2)}) %all-to-all-start.6) | async-done | bytes 884768 | tf_op jit(solution)/shard_map/all_to_all | solution.py:432
  345.4 65.3 %attend_pull.1 = (bf16[2304,192]{1,0:T(8,128)(2,1)}, bf16[4608,384]{1,0:T(8,128)(2,1)}) custom-call(s32[2,8]{1,0:T(2,128)} %pad_add_fusion.span_ref, bf16[2304,192]{1,0:T(8,128)(2,1)} %bitcast.207, s32[2304,128]{1,0:T(8,128)} %broadcast_in_dim.38.qid_ref, s32[1,1,4608]{2,1,0:T(1,128)} %get-tuple-element.123.kid_ref, bf16[4608,384]{1,0:T(8,128)(2,1)} %bitcast.187, ...), custom_call_target="tpu_custom_call" | custom-call | tf_op jit(solution)/shard_map/attend_pull/pallas_call | solution.py:208
  410.7 4.4 copy.179
  417.9 4.9 pad_maximum_fusion.2
  422.7 7.0 %all-to-all-start.7 = ((bf16[8,720,384]{2,1,0:T(8,128)(2,1)}), bf16[8,720,384]{2,1,0:T(8,128)(2,1)}, u32[]{:S(2)}, u32[]{:S(2)}) async-start(bf16[8,720,384]{2,1,0:T(8,128)(2,1)} %pad_maximum_fusion.2), calls=%async_computation.7 | async-start | bytes 8847360 | tf_op jit(solution)/shard_map/all_to_all | solution.py:432
  435.2 10.6 %copy.181 = bf16[768,4608]{1,0:T(8,128)(2,1)} copy(bf16[768,4608]{0,1:T(8,128)(2,1)} %bitcast.210) | data formatting | bytes 14155776 | tf_op jit(solution)/shard_map/dot_general | solution.py:27
  445.8 5.1 convolution_convert_fusion.1
  456.8 30.6 %all-to-all-done.7 = bf16[8,720,384]{2,1,0:T(8,128)(2,1)} async-done(((bf16[8,720,384]{2,1,0:T(8,128)(2,1)}), bf16[8,720,384]{2,1,0:T(8,128)(2,1)}, u32[]{:S(2)}, u32[]{:S(2)}) %all-to-all-start.7) | async-done | bytes 4423712 | tf_op jit(solution)/shard_map/all_to_all | solution.py:432
  487.5 14.0 %all-to-all-start.5 = ((bf16[4,144,768]{2,1,0:T(8,128)(2,1)}), bf16[4,144,768]{2,1,0:T(8,128)(2,1)S(1)}, u32[]{:S(2)}, u32[]{:S(2)}) async-start(bf16[4,144,768]{2,1,0:T(8,128)(2,1)} %bitcast.44), calls=%async_computation.5 | async-start | bytes 1769472 | tf_op jit(solution)/shard_map/all_to_all | solution.py:463
  518.9 10.7 %all-to-all-done.5 = bf16[4,144,768]{2,1,0:T(8,128)(2,1)S(1)} async-done(((bf16[4,144,768]{2,1,0:T(8,128)(2,1)}), bf16[4,144,768]{2,1,0:T(8,128)(2,1)S(1)}, u32[]{:S(2)}, u32[]{:S(2)}) %all-to-all-start.5) | async-done | bytes 884768 | tf_op jit(solution)/shard_map/all_to_all | solution.py:463
  529.6 5.5 all-to-all-start.9
  535.2 6.0 fusion.13
  548.5 10.7 %all-to-all-done.9 = bf16[8,96,576]{2,1,0:T(8,128)(2,1)} async-done(((bf16[8,96,576]{2,1,0:T(8,128)(2,1)}), bf16[8,96,576]{2,1,0:T(8,128)(2,1)}, u32[]{:S(2)}, u32[]{:S(2)}) %all-to-all-start.9) | async-done | bytes 884768 | tf_op jit(solution)/shard_map/all_to_all | solution.py:495
  566.7 4.3 all-to-all-done.10
  579.6 17.6 %all-to-all-done.8 = bf16[4,144,768]{2,1,0:T(8,128)(2,1)S(1)} async-done(((bf16[4,144,768]{2,1,0:T(8,128)(2,1)}), bf16[4,144,768]{2,1,0:T(8,128)(2,1)S(1)}, u32[]{:S(2)}, u32[]{:S(2)}) %all-to-all-start.8) | async-done | bytes 884768 | tf_op jit(solution)/shard_map/all_to_all | solution.py:485
  (257 shorter events, 144.5 us)
Async XLA Ops:
  7.2 19.7 %copy-start.19 = (bf16[4,144,768]{2,1,0:T(8,128)(2,1)S(1)}, bf16[4,144,768]{2,1,0:T(8,128)(2,1)}, u32[]{:S(2)}) copy-start(bf16[4,144,768]{2,1,0:T(8,128)(2,1)} %param.11) | copy-start | bytes 2654212
  7.2 89.4 %all-gather.4.cloned.1.call-start = ((), (), s32[]{:S(2)}) async-start(), calls=%async_computation.12 | async-start | bytes 4055040 | tf_op jit(solution)/shard_map/all_gather | solution.py:359
  26.9 34.6 %copy-start.27 = (bf16[192,96]{1,0:T(8,128)(2,1)S(1)}, bf16[192,96]{1,0:T(8,128)(2,1)}, u32[]{:S(2)}) copy-start(bf16[192,96]{1,0:T(8,128)(2,1)} %param.15) | copy-start | bytes 110596
  26.9 34.7 %copy-start.20 = (bf16[768,96]{0,1:T(8,128)(2,1)S(1)}, bf16[768,96]{0,1:T(8,128)(2,1)}, u32[]{:S(2)}) copy-start(bf16[768,96]{0,1:T(8,128)(2,1)} %param.18) | copy-start | bytes 442372
  26.9 34.7 %copy-start.21 = (bf16[96,768]{1,0:T(8,128)(2,1)S(1)}, bf16[96,768]{1,0:T(8,128)(2,1)}, u32[]{:S(2)}) copy-start(bf16[96,768]{1,0:T(8,128)(2,1)} %param.16) | copy-start | bytes 442372
  57.9 34.5 %all-to-all-start.1 = ((bf16[4,144,768]{2,1,0:T(8,128)(2,1)}), bf16[4,144,768]{2,1,0:T(8,128)(2,1)S(1)}, u32[]{:S(2)}, u32[]{:S(2)}) async-start(bf16[4,144,768]{2,1,0:T(8,128)(2,1)} %param.21), calls=%async_computation.1 | async-start | bytes 1769472 | tf_op jit(solution)/shard_map/all_to_all | solution.py:366
  61.4 213.9 %all-gather.6.cloned.1.call-start = ((), (), s32[]{:S(2)}) async-start(), calls=%async_computation.13 | async-start | bytes 11354112 | tf_op jit(solution)/shard_map/all_gather | solution.py:369
  110.1 85.2 %all-to-all-start.3 = ((bf16[8,720,384]{2,1,0:T(8,128)(2,1)}), bf16[8,720,384]{2,1,0:T(8,128)(2,1)}, u32[]{:S(2)}, u32[]{:S(2)}) async-start(bf16[8,720,384]{2,1,0:T(8,128)(2,1)} %pad_maximum_fusion.1), calls=%async_computation.3 | async-start | bytes 8847360 | tf_op jit(solution)/shard_map/all_to_all | solution.py:432
  114.7 320.5 %all-gather.8.cloned.1.call-start = ((), (), s32[]{:S(2)}) async-start(), calls=%async_computation.14 | async-start | bytes 7962624 | tf_op jit(solution)/shard_map/all_gather | solution.py:453
  273.7 4.6 copy-start.4
  315.5 5.3 copy-start.1
  326.4 17.1 %all-to-all-start.6 = ((bf16[8,144,384]{2,1,0:T(8,128)(2,1)}), bf16[8,144,384]{2,1,0:T(8,128)(2,1)S(1)}, u32[]{:S(2)}, u32[]{:S(2)}) async-start(bf16[8,144,384]{2,1,0:T(8,128)(2,1)} %reshape_reshape.22), calls=%async_computation.6 | async-start | bytes 1769472 | tf_op jit(solution)/shard_map/all_to_all | solution.py:432
  330.0 267.2 %reduce-scatter.2.cloned.1.call-start = ((), (), s32[]{:S(2)}) async-start(), calls=%async_computation.15 | async-start | bytes 11354112 | tf_op jit(solution)/shard_map/reduce_scatter | solution.py:471
  422.7 9.9 %copy-start.29 = (f32[4,1,768]{2,1,0:T(1,128)S(1)}, f32[4,1,768]{2,1,0:T(1,128)}, u32[]{:S(2)}) copy-start(f32[4,1,768]{2,1,0:T(1,128)} %get-tuple-element.40) | copy-start | bytes 36868
  422.7 64.7 %all-to-all-start.7 = ((bf16[8,720,384]{2,1,0:T(8,128)(2,1)}), bf16[8,720,384]{2,1,0:T(8,128)(2,1)}, u32[]{:S(2)}, u32[]{:S(2)}) async-start(bf16[8,720,384]{2,1,0:T(8,128)(2,1)} %pad_maximum_fusion.2), calls=%async_computation.7 | async-start | bytes 8847360 | tf_op jit(solution)/shard_map/all_to_all | solution.py:432
  435.2 10.6 %copy-start.17 = (bf16[2,4,2,2,144,192]{5,4,3,2,1,0:T(8,128)(2,1)S(1)}, bf16[2,4,2,2,144,192]{5,4,3,2,1,0:T(8,128)(2,1)}, u32[]{:S(2)}) copy-start(bf16[2,4,2,2,144,192]{5,4,3,2,1,0:T(8,128)(2,1)} %broadcast_select_fusion) | copy-start | bytes 5308420
  445.8 5.2 copy-start.3
  445.8 6.1 %copy-start.7 = (bf16[768,4608]{1,0:T(8,128)(2,1)S(1)}, bf16[768,4608]{1,0:T(8,128)(2,1)}, u32[]{:S(2)}) copy-start(bf16[768,4608]{1,0:T(8,128)(2,1)} %copy.181) | copy-start | bytes 21233668
  487.5 42.2 %all-to-all-start.5 = ((bf16[4,144,768]{2,1,0:T(8,128)(2,1)}), bf16[4,144,768]{2,1,0:T(8,128)(2,1)S(1)}, u32[]{:S(2)}, u32[]{:S(2)}) async-start(bf16[4,144,768]{2,1,0:T(8,128)(2,1)} %bitcast.44), calls=%async_computation.5 | async-start | bytes 1769472 | tf_op jit(solution)/shard_map/all_to_all | solution.py:463
  508.2 8.6 %copy-start = (bf16[4,2,2,144,192]{4,3,2,1,0:T(8,128)(2,1)}, bf16[4,2,2,144,192]{4,3,2,1,0:T(8,128)(2,1)S(1)}, u32[]{:S(2)}) copy-start(bf16[4,2,2,144,192]{4,3,2,1,0:T(8,128)(2,1)S(1)} %copy.180) | copy-start | bytes 2654212
  529.6 29.6 %all-to-all-start.9 = ((bf16[8,96,576]{2,1,0:T(8,128)(2,1)}), bf16[8,96,576]{2,1,0:T(8,128)(2,1)}, u32[]{:S(2)}, u32[]{:S(2)}) async-start(bf16[8,96,576]{2,1,0:T(8,128)(2,1)} %pad_maximum_fusion.7), calls=%async_computation.9 | async-start | bytes 1966080 | tf_op jit(solution)/shard_map/all_to_all | solution.py:495
  535.2 10.3 %slice-start = ((f32[4,576]{1,0:T(4,128)}), f32[4,192]{1,0:T(4,128)S(1)}, s32[]{:S(2)}) async-start(f32[4,576]{1,0:T(4,128)} %copy-done.28), calls=%async_computation.16 | async-start | bytes 8192 | tf_op jit(solution)/shard_map/slice | solution.py:502
  559.2 11.7 %all-to-all-start.10 = ((f32[32,8,128]{2,1,0:T(8,128)}), f32[32,8,128]{2,1,0:T(8,128)S(1)}, u32[]{:S(2)}, u32[]{:S(2)}) async-start(f32[32,8,128]{2,1,0:T(8,128)} %bitcast.101), calls=%async_computation.10 | async-start | bytes 262144 | tf_op jit(solution)/shard_map/all_to_all | solution.py:517
  570.9 26.2 %all-to-all-start.8 = ((bf16[4,144,768]{2,1,0:T(8,128)(2,1)}), bf16[4,144,768]{2,1,0:T(8,128)(2,1)S(1)}, u32[]{:S(2)}, u32[]{:S(2)}) async-start(bf16[4,144,768]{2,1,0:T(8,128)(2,1)} %bitcast.64), calls=%async_computation.8 | async-start | bytes 1769472 | tf_op jit(solution)/shard_map/all_to_all | solution.py:485
  (19 other events, 43.4 us)
Sparse Core Ops, SparseCore 0:
  11.5 72.5 all-gather.3
  92.5 114.2 all-gather.5
  273.8 45.8 all-gather.7
  345.5 185.1 reduce-scatter.1

commit v4 on v3

--- a/solution.py
+++ b/solution.py
@@ -333,6 +333,26 @@
     return (t - jnp.mean(t, axis=-1, keepdims=True) - hat * jnp.mean(t * hat, axis=-1, keepdims=True)) * inverse
 
 
+def gather_plane(a, my_part, my_mp):
+    rows, width = a.shape
+    half = rows // 2
+
+    def move(v, dy, dm):
+        pairs = [(p * 4 + m, (p ^ dy) * 4 + (m ^ dm)) for p in range(2) for m in range(4)]
+        return lax.ppermute(v, PLANE, pairs)
+
+    beside = move(a, 0, 2)
+    above = move(a, 1, 0)
+    low = move(beside[:half], 1, 0)
+    high = move(above[half:], 0, 2)
+    same = [(0, 0, 0, a), (0, 2, 0, beside), (1, 0, 0, above), (1, 2, 0, low), (1, 2, half, high)]
+    pieces = same + [(dy, dm ^ 1, at, move(v, 0, 1)) for dy, dm, at, v in same]
+    out = jnp.zeros((2, 4, rows, width), a.dtype)
+    for dy, dm, at, v in pieces:
+        out = lax.dynamic_update_slice(out, v[None, None], (my_part ^ dy, my_mp ^ dm, at, 0))
+    return out.reshape(8 * rows, width)
+
+
 def local(frames, clip_ids, w_qkv, b_qv, w_out, w_up, b_up, w_down, gains, biases, cotangent):
     mbs, share, width = frames.shape
     mp = lax.axis_size("mp")
@@ -349,6 +369,7 @@
     my_part = lax.axis_index("part")
     my_mp = lax.axis_index("mp")
     flip = (my_mp // 2) % 2 == 1
+    flat = parts == 2 and mp == 4
 
     wide = 3 * head_cols
     kv_cols = 2 * head_cols
@@ -356,19 +377,20 @@
         [w_qkv[:, 1].reshape(band, heads, HD), w_qkv[:, 2].reshape(band, heads, HD)], axis=2
     ).reshape(band, kv_cols)
     shard_one = jnp.concatenate([kv_shard, w_qkv[:, 0]], axis=1)
-    got_one = lax.all_gather(shard_one, OWNER, axis=0, tiled=True)
+    if flat:
+        weight_own = lax.all_gather(shard_one, ("mb", "part"), axis=0, tiled=True)
+    else:
+        weight_qkv = lax.all_gather(shard_one, OWNER, axis=0, tiled=True).reshape(mp, width, wide)
     smalls = (b_qv, b_up, gains, biases)
     small_sizes = [a.size for a in smalls]
     line = jnp.concatenate([a.reshape(-1) for a in smalls])
     line = jnp.pad(line, (0, 1024 - line.shape[0])).reshape(1, 8, 128)
     lines = lax.all_to_all(jnp.broadcast_to(line, (mp * dp, 8, 128)), OWNER, 0, 0, tiled=True)
     x_bf = lax.all_to_all(frames, "mb", 0, 0, tiled=True).reshape(rows, width)
-    g_bf = lax.all_to_all(cotangent, "mb", 0, 0, tiled=True).reshape(rows, width)
     shard_two = jnp.concatenate([w_up, w_down.T, w_out.T], axis=1)
-    shard_two, x_bf, g_bf, lines = lax.optimization_barrier((shard_two, x_bf, g_bf, lines))
+    shard_two, x_bf, lines = lax.optimization_barrier((shard_two, x_bf, lines))
     got_two = lax.all_gather(shard_two, OWNER, axis=0, tiled=True).reshape(mp, width, 2 * ff + head_cols)
 
-    weight_qkv = got_one.reshape(mp, width, wide)
     lines = lines.reshape(mp, dp, 1024).astype(f32)
     cuts = []
     at = 0
@@ -438,19 +460,33 @@
     bias_v = bias_qv[1].reshape(mp, heads, 1, HD)
     bias_kv = jnp.concatenate([jnp.zeros_like(bias_v), bias_v], axis=2).reshape(mp, 2 * head_cols)
     bias_all = jnp.concatenate([bias_kv, bias_q], axis=1)
-    proj = jnp.stack([(dot(h1, weight_qkv[m]) + bias_all[m]).astype(bf16) for m in range(mp)])
-    kv_part = jnp.broadcast_to(proj[None, :, :, :kv_cols], (parts, mp, rows, 2 * head_cols))
-    sent = jnp.concatenate([to_parts(proj[:, :, kv_cols:]), kv_part], axis=2)
-    came = swap(sent)
-    q_tiles = to_tiles(came[:, :, :half])
-    kv_seq = (
-        came[:, :, half:].reshape(parts, mp, mbs, share, 2 * head_cols).transpose(2, 0, 1, 3, 4).reshape(seq, 2 * head_cols)
-    )
+    if flat:
+        h1_plane = gather_plane(h1, my_part, my_mp)
+        bias_own = lax.dynamic_index_in_dim(bias_all, my_mp, 0)
+        kv_own = (dot(h1_plane, weight_own[:, :kv_cols]) + bias_own[:, :kv_cols]).astype(bf16)
+        kv_seq = kv_own.reshape(parts, mp, mbs, share, kv_cols).transpose(2, 0, 1, 3, 4).reshape(seq, kv_cols)
+        q_own = (dot(h1_plane, weight_own[:, kv_cols:]) + bias_own[:, kv_cols:]).astype(bf16)
+        q_own = q_own.reshape(parts, mp, 2, 2, share, head_cols)
+        spot = ((jnp.arange(mp) // 2 + my_part) % 2 == 1)[None, :, None, None, None]
+        q_tiles = jnp.where(spot, q_own[:, :, :, 1], q_own[:, :, :, 0])
+        q_tiles = q_tiles.transpose(2, 0, 1, 3, 4).reshape(-1, head_cols)
+        g_in = lax.optimization_barrier((cotangent, kv_seq))
+        kv_seq = g_in[1]
+        g_bf = lax.all_to_all(g_in[0], "mb", 0, 0, tiled=True).reshape(rows, width)
+    else:
+        proj = jnp.stack([(dot(h1, weight_qkv[m]) + bias_all[m]).astype(bf16) for m in range(mp)])
+        kv_part = jnp.broadcast_to(proj[None, :, :, :kv_cols], (parts, mp, rows, kv_cols))
+        came = swap(jnp.concatenate([to_parts(proj[:, :, kv_cols:]), kv_part], axis=2))
+        q_tiles = to_tiles(came[:, :, :half])
+        kv_seq = (
+            came[:, :, half:].reshape(parts, mp, mbs, share, kv_cols).transpose(2, 0, 1, 3, 4).reshape(seq, kv_cols)
+        )
+        g_bf = lax.all_to_all(cotangent, "mb", 0, 0, tiled=True).reshape(rows, width)
     att_tiles, lse = attend(span, q_tiles, qid, kid, kv_seq, heads, block)
     att = from_parts(swap(from_tiles(att_tiles)))
-    if parts == 2:
-        h1_late, att = lax.optimization_barrier((h1, att))
-        h1_plane = lax.all_gather(h1_late, PLANE, axis=0, tiled=True)
+    if flat:
+        own_late, att = lax.optimization_barrier((weight_own, att))
+        weight_qkv = lax.all_gather(own_late, "mp", axis=0, tiled=True).reshape(mp, width, wide)
     mixed = x + bias_rows[1]
     for m in range(mp):
         mixed = mixed + dot(att[m], weight_out[m], NT)
@@ -467,7 +503,7 @@
     datt = jnp.stack([dot(drb, weight_out[m]).astype(bf16) for m in range(mp)])
     datt_tiles = to_tiles(swap(to_parts(datt)))
     grads_two = out_grads(drb, att, grads_two, 2 * ff)
-    datt_tiles, grads_two = lax.optimization_barrier((datt_tiles, grads_two))
+    datt_tiles, grads_two, output = lax.optimization_barrier((datt_tiles, grads_two, output))
     mine_two = lax.psum_scatter(
         grads_two.reshape(mp * width, grad_wide), OWNER, scatter_dimension=0, tiled=True
     ).astype(f32)
@@ -475,6 +511,17 @@
     dq_tiles, dkv_seq = attend_pull(span, q_tiles, qid, kid, kv_seq, datt_tiles, att_tiles, lse, heads, block)
     dkv_sent = dkv_seq.reshape(mbs, parts, mp, share, 2 * head_cols).transpose(1, 2, 0, 3, 4).reshape(parts, mp, rows, 2 * head_cols)
     back = swap(jnp.concatenate([from_tiles(dq_tiles), dkv_sent], axis=2))
+    if flat:
+        spot = (jnp.arange(mp)[None] // 2 + my_part) % 2 == jnp.arange(2)[:, None]
+        own = dq_tiles.reshape(2, parts, mp, 1, share, head_cols).transpose(1, 2, 0, 3, 4, 5)
+        own = jnp.where(spot.T[None, :, None, :, None, None], own, bf16(0)).reshape(parts * mp * rows, head_cols)
+        part_qkv = jnp.concatenate(
+            [dot(h1_plane, dkv_sent.reshape(parts * mp * rows, kv_cols), TN), dot(h1_plane, own, TN)], axis=1
+        )
+        part_qkv = part_qkv.astype(bf16).reshape(dp, band, wide)
+        part_qkv = lax.all_to_all(part_qkv, ("mb", "part"), 0, 0, tiled=True)
+        back, part_qkv = lax.optimization_barrier((back, part_qkv))
+        mine_one = jnp.sum(part_qkv, axis=0, dtype=f32)
     dq = from_parts(back[:, :, :half])
     dkv = jnp.sum(back[:, :, half:], axis=0, dtype=f32).astype(bf16)
     dproj = jnp.concatenate([dkv, dq], axis=2)
@@ -484,16 +531,7 @@
     dx = (dr1 + norm_pull(grad_one, hat_one, inv_one, gain_rows[0])).astype(bf16)
     frames_grad = lax.all_to_all(dx.reshape(mbs, share, width), "mb", 0, 0, tiled=True)
 
-    if parts == 2:
-        spot = (jnp.arange(mp)[None] // 2 + my_part) % 2 == jnp.arange(2)[:, None]
-        own = dq_tiles.reshape(2, parts, mp, 1, share, head_cols).transpose(1, 2, 0, 3, 4, 5)
-        own = jnp.where(spot.T[None, :, None, :, None, None], own, bf16(0)).reshape(parts * mp * rows, head_cols)
-        part_qkv = jnp.concatenate(
-            [dot(h1_plane, dkv_sent.reshape(parts * mp * rows, kv_cols), TN), dot(h1_plane, own, TN)], axis=1
-        )
-        part_qkv = part_qkv.astype(bf16).reshape(dp, band, wide)
-        mine_one = jnp.sum(lax.all_to_all(part_qkv, ("mb", "part"), 0, 0, tiled=True), axis=0, dtype=f32)
-    else:
+    if not flat:
         grads_qkv = jnp.stack([dot(h1, dproj[m], TN).astype(bf16) for m in range(mp)])
         spans = grads_qkv.reshape(mp, mbs, parts, band, wide).transpose(2, 0, 1, 3, 4)
         plane_sum = jnp.sum(swap(spans).reshape(parts * mp, mbs, band, wide), axis=0, dtype=f32).astype(bf16)

time: 617 us -> 619 us (level)
  waiting for transfers between devices: 189 us -> 165 us
  blocking collectives: 63.9 us -> 87.1 us
    all_to_all x3 -> x2, waiting for transfers between devices: 116 us -> 61.4 us  [swap(): lax.all_to_all(a.reshape((parts * mp,) + a.shape[2:]), PLANE, 0, 0, tiled...]
    all_gather x0 -> x1, blocking collectives: none -> 54.2 us  [local(): weight_own = lax.all_gather(shard_one, ('mb', 'part'), axis=0, tiled=True)]
    all_to_all x1 -> x0, blocking collectives: 31 us -> none  [local(): x_bf = lax.all_to_all(frames, 'mb', 0, 0, tiled=True).reshape(rows, width)]
    ppermute x0 -> x9, waiting for transfers between devices: none -> 16.6 us  [move(): return lax.ppermute(v, PLANE, pairs)]
    all_to_all x2 -> x3, waiting for transfers between devices: 40.7 us -> 52.4 us  [the longest x1 24.4 us: local(): part_qkv = lax.all_to_all(part_qkv, ('mb', 'part'), 0, 0, tiled=True)]
    all_to_all x2 -> x3, starting transfers between devices: 9.03 us -> 20.4 us  [the longest x1 13 us: local(): part_qkv = lax.all_to_all(part_qkv, ('mb', 'part'), 0, 0, tiled=True)]
    dynamic_update_slice x0 -> x9, local copies, waits for them, and re-layouts: none -> 10.6 us  [gather_plane(): lax.dynamic_update_slice(out, v[None, None], (my_part ^ dy, my_mp ^ dm, a...]
    all_to_all x1, starting transfers between devices: 14 us -> 4.23 us  [local(): lax.all_to_all(result.astype(bf16).reshape(mbs, share, width), 'mb', 0, 0...]
  transfers between devices with their start and end apart: 12 -> 20, of which waited for: 8 -> 9; matrix products, arithmetic and copies ran while one was open for 25% -> 24% of each run, Pallas kernels for 22% -> 23%
where the time goes in v4:
time: 619 us; the launch traced here: 616 us
  waiting for transfers between devices  165 us (27%)
  Pallas kernels  140 us (23%)
  blocking collectives  87.1 us (14%)
  local copies, waits for them, and re-layouts  82.2 us (13%)
  starting transfers between devices  48.5 us (8%)
  matrix products  40.6 us (7%)
  other arithmetic  37.4 us (6%)
  between operations  15.1 us (2%)
    pallas_call x1, Pallas kernels, attend_pull(): pl.pallas_call(functools.partial(pull_kernel, heads=heads, block=block),...  69.3 us
    all_to_all x2, waiting for transfers between devices, swap(): lax.all_to_all(a.reshape((parts * mp,) + a.shape[2:]), PLANE, 0, 0, tiled...  61.4 us
    all_gather x1, blocking collectives, local(): weight_own = lax.all_gather(shard_one, ('mb', 'part'), axis=0, tiled=True)  54.2 us
    pallas_call x1, Pallas kernels, attend(): pl.pallas_call(functools.partial(attend_kernel, heads=heads, block=block)...  40.6 us
    dot_general x16, matrix products, dot(): return lax.dot_general(a, b, dims, preferred_element_type=f32)  40.6 us
    pallas_call x1, Pallas kernels, feed_forward(): pl.pallas_call(functools.partial(feed_kernel, ff=ff), grid=(mp,), in_spec...  25.2 us
    all_to_all x1, waiting for transfers between devices, local(): part_qkv = lax.all_to_all(part_qkv, ('mb', 'part'), 0, 0, tiled=True)  24.4 us
    all_to_all x1, waiting for transfers between devices, local(): x_bf = lax.all_to_all(frames, 'mb', 0, 0, tiled=True).reshape(rows, width)  21.8 us
  transfers between devices with their start and end apart: 20, of which 9 were waited for; matrix products, arithmetic and copies ran while one was open for 24% of the time, Pallas kernels for 23%

profile of v4, /device:TPU:0, one launch (start us, length us, event | category | flops | bytes accessed | tf_op | source)
XLA Modules:
  0.0 616.0 jit_solution(5526429952997352083)
XLA Ops:
  10.3 14.4 %all_to_all.50 = bf16[32,8,128]{2,1,0:T(8,128)(2,1)S(1)} all-to-all(bf16[32,8,128]{2,1,0:T(8,128)(2,1)S(1)} %broadcast_in_dim.105), channel_id=1, replica_groups=mesh['mb'=4,'part'=2,'mp'=4] {'mp','mb','part'}, dimensions={0} | all-to-all | bytes 131072 | tf_op jit(solution)/shard_map/all_to_all | solution.py:388
  29.1 21.8 %all-to-all-done = bf16[4,144,768]{2,1,0:T(8,128)(2,1)S(1)} async-done(((bf16[4,144,768]{2,1,0:T(8,128)(2,1)}), bf16[4,144,768]{2,1,0:T(8,128)(2,1)S(1)}, u32[]{:S(2)}, u32[]{:S(2)}) %all-to-all-start) | async-done | bytes 884768 | tf_op jit(solution)/shard_map/all_to_all | solution.py:389
  62.8 54.2 %all_gather.9 = bf16[768,576]{1,0:T(8,128)(2,1)S(1)} all-gather(bf16[96,576]{1,0:T(8,128)(2,1)S(1)} %copy.158), channel_id=1, replica_groups=mesh['mb'=4,'part'=2,'mp'=4] {'mb','part'}, dimensions={0}, use_global_device_ids=true | all-gather | bytes 995328 | tf_op jit(solution)/shard_map/all_gather | solution.py:381
  124.1 16.6 %collective-permute-done.2 = bf16[288,768]{1,0:T(8,128)(2,1)S(1)} collective-permute-done((bf16[288,768]{1,0:T(8,128)(2,1)S(1)}, bf16[288,768]{1,0:T(8,128)(2,1)S(1)}, u32[]{:S(2)}, u32[]{:S(2)}) %collective-permute-start.2) | collective-permute-done | bytes 442400 | tf_op jit(solution)/shard_map/ppermute | solution.py:342
  148.6 6.9 %fusion.1 = bf16[4608,192]{0,1:T(8,128)(2,1)} fusion(bf16[4608,768]{1,0:T(8,128)(2,1)} %bitcast.17, f32[192]{0:T(256)S(1)} %bitcast.260, bf16[768,576]{1,0:T(8,128)(2,1)S(1)} %all_gather.9), kind=kOutput, calls=%fused_computation.3 | convolution fusion | flops 1360723968 | bytes 9241600 | tf_op jit(solution)/shard_map/dot_general | solution.py:27
  160.0 6.9 %fusion = bf16[4608,384]{1,0:T(8,128)(2,1)S(1)} fusion(bf16[4608,768]{1,0:T(8,128)(2,1)} %bitcast.17, f32[384]{0:T(512)S(1)} %slice_reduce_fusion.4, bf16[768,576]{1,0:T(8,128)(2,1)S(1)} %copy-done.12), kind=kOutput, calls=%fused_computation.1 | convolution fusion | flops 2721447936 | bytes 11208704 | tf_op jit(solution)/shard_map/dot_general | solution.py:27
  170.9 40.6 %attend.1 = (bf16[2304,192]{1,0:T(8,128)(2,1)}, f32[3,2304,128]{2,1,0:T(8,128)}) custom-call(s32[2,8]{1,0:T(2,128)} %pad_add_fusion.span_ref, bf16[2304,192]{1,0:T(8,128)(2,1)} %bitcast.227, s32[2304,128]{1,0:T(8,128)} %broadcast_in_dim.119.qid_ref, s32[1,1,4608]{2,1,0:T(1,128)} %get-tuple-element.128.kid_ref, bf16[4608,384]{1,0:T(8,128)(2,1)} %bitcast.208), custom_call_target="tpu_custom_call" | custom-call | tf_op jit(solution)/shard_map/attend/pallas_call | solution.py:122
  215.5 8.3 %all-to-all-start.3 = ((bf16[8,144,384]{2,1,0:T(8,128)(2,1)}), bf16[8,144,384]{2,1,0:T(8,128)(2,1)S(1)}, u32[]{:S(2)}, u32[]{:S(2)}) async-start(bf16[8,144,384]{2,1,0:T(8,128)(2,1)} %reshape_reshape.20), calls=%async_computation.3 | async-start | bytes 1769472 | tf_op jit(solution)/shard_map/all_to_all | solution.py:454
  226.6 10.8 %all-to-all-done.3 = bf16[8,144,384]{2,1,0:T(8,128)(2,1)S(1)} async-done(((bf16[8,144,384]{2,1,0:T(8,128)(2,1)}), bf16[8,144,384]{2,1,0:T(8,128)(2,1)S(1)}, u32[]{:S(2)}, u32[]{:S(2)}) %all-to-all-start.3) | async-done | bytes 884768 | tf_op jit(solution)/shard_map/all_to_all | solution.py:454
  254.8 6.2 %all-to-all-done.2 = bf16[4,144,768]{2,1,0:T(8,128)(2,1)S(1)} async-done(((bf16[4,144,768]{2,1,0:T(8,128)(2,1)}), bf16[4,144,768]{2,1,0:T(8,128)(2,1)S(1)}, u32[]{:S(2)}, u32[]{:S(2)}) %all-to-all-start.2) | async-done | bytes 884768 | tf_op jit(solution)/shard_map/all_to_all | solution.py:475
  261.9 25.2 %feed_forward.1 = (f32[576,768]{1,0:T(8,128)}, f32[576,768]{1,0:T(8,128)}, bf16[4,768,1792]{2,1,0:T(8,128)(2,1)}, f32[4,1,768]{2,1,0:T(1,128)}) custom-call(bf16[576,768]{1,0:T(8,128)(2,1)} %add_convert_fusion.1.h2_ref, bf16[576,768]{1,0:T(8,128)(2,1)} %bitcast.219, bf16[4,768,1728]{2,1,0:T(8,128)(2,1)} %bitcast.214, f32[4,1,768]{2,1,0:T(1,128)} %reshape.470.b_ref), custom_call_target="tpu_custom_call" | custom-call | tf_op jit(solution)/shard_map/feed_forward/pallas_call | solution.py:273
  309.5 18.4 %all_to_all.51 = bf16[8,144,384]{2,1,0:T(8,128)(2,1)} all-to-all(bf16[8,144,384]{2,1,0:T(8,128)(2,1)} %reshape_reshape.22), channel_id=1, replica_groups=mesh['mb'=4,'part'=2,'mp'=4] {'part','mp'}, dimensions={0} | all-to-all | bytes 1769472 | tf_op jit(solution)/shard_map/all_to_all | solution.py:454
  327.9 4.2 all-to-all-start.5
  332.2 5.1 out_grads.1
  341.8 12.6 %all-to-all-done.5 = bf16[4,144,768]{2,1,0:T(8,128)(2,1)} async-done(((bf16[4,144,768]{2,1,0:T(8,128)(2,1)}), bf16[4,144,768]{2,1,0:T(8,128)(2,1)}, u32[]{:S(2)}, u32[]{:S(2)}) %all-to-all-start.5) | async-done | bytes 884768 | tf_op jit(solution)/shard_map/all_to_all | solution.py:499
  354.6 10.5 %copy.182 = bf16[768,4608]{1,0:T(8,128)(2,1)} copy(bf16[768,4608]{0,1:T(8,128)(2,1)} %bitcast.65) | data formatting | bytes 14155776 | tf_op jit(solution)/shard_map/dot_general | solution.py:27
  365.1 69.3 %attend_pull.1 = (bf16[2304,192]{1,0:T(8,128)(2,1)}, bf16[4608,384]{1,0:T(8,128)(2,1)}) custom-call(s32[2,8]{1,0:T(2,128)} %pad_add_fusion.span_ref, bf16[2304,192]{1,0:T(8,128)(2,1)} %bitcast.228, s32[2304,128]{1,0:T(8,128)} %broadcast_in_dim.119.qid_ref, s32[1,1,4608]{2,1,0:T(1,128)} %get-tuple-element.128.kid_ref, bf16[4608,384]{1,0:T(8,128)(2,1)} %bitcast.209, ...), custom_call_target="tpu_custom_call" | custom-call | tf_op jit(solution)/shard_map/attend_pull/pallas_call | solution.py:208
  447.6 13.0 %all-to-all-start.7 = ((bf16[8,96,576]{2,1,0:T(8,128)(2,1)}), bf16[8,96,576]{2,1,0:T(8,128)(2,1)}, u32[]{:S(2)}, u32[]{:S(2)}) async-start(bf16[8,96,576]{2,1,0:T(8,128)(2,1)} %pad_maximum_fusion.2), calls=%async_computation.7 | async-start | bytes 1966080 | tf_op jit(solution)/shard_map/all_to_all | solution.py:522
  464.6 4.7 pad_maximum_fusion.1
  469.3 24.4 %all-to-all-done.7 = bf16[8,96,576]{2,1,0:T(8,128)(2,1)} async-done(((bf16[8,96,576]{2,1,0:T(8,128)(2,1)}), bf16[8,96,576]{2,1,0:T(8,128)(2,1)}, u32[]{:S(2)}, u32[]{:S(2)}) %all-to-all-start.7) | async-done | bytes 884768 | tf_op jit(solution)/shard_map/all_to_all | solution.py:522
  493.8 4.9 all-to-all-start.6
  499.4 50.6 %all-to-all-done.6 = bf16[8,720,384]{2,1,0:T(8,128)(2,1)} async-done(((bf16[8,720,384]{2,1,0:T(8,128)(2,1)}), bf16[8,720,384]{2,1,0:T(8,128)(2,1)}, u32[]{:S(2)}, u32[]{:S(2)}) %all-to-all-start.6) | async-done | bytes 4423712 | tf_op jit(solution)/shard_map/all_to_all | solution.py:454
  572.4 4.2 all-to-all-done.9
  585.3 17.6 %all-to-all-done.8 = bf16[4,144,768]{2,1,0:T(8,128)(2,1)S(1)} async-done(((bf16[4,144,768]{2,1,0:T(8,128)(2,1)}), bf16[4,144,768]{2,1,0:T(8,128)(2,1)S(1)}, u32[]{:S(2)}, u32[]{:S(2)}) %all-to-all-start.8) | async-done | bytes 884768 | tf_op jit(solution)/shard_map/all_to_all | solution.py:532
  (279 shorter events, 149.4 us)
Async XLA Ops:
  7.2 43.7 %copy-start.15 = (bf16[96,3,192]{2,0,1:T(8,128)(2,1)S(1)}, bf16[96,3,192]{2,0,1:T(8,128)(2,1)}, u32[]{:S(2)}) copy-start(bf16[96,3,192]{2,0,1:T(8,128)(2,1)} %param.13) | copy-start | bytes 331780
  24.7 26.3 %all-to-all-start = ((bf16[4,144,768]{2,1,0:T(8,128)(2,1)}), bf16[4,144,768]{2,1,0:T(8,128)(2,1)S(1)}, u32[]{:S(2)}, u32[]{:S(2)}) async-start(bf16[4,144,768]{2,1,0:T(8,128)(2,1)} %param.11), calls=%async_computation | async-start | bytes 1769472 | tf_op jit(solution)/shard_map/all_to_all | solution.py:389
  28.2 217.8 %all-gather.3.cloned.1.call-start = ((), (), s32[]{:S(2)}) async-start(), calls=%async_computation.11 | async-start | bytes 11354112 | tf_op jit(solution)/shard_map/all_gather | solution.py:392
  60.3 57.3 %collective-permute-start = (bf16[576,768]{1,0:T(8,128)(2,1)}, bf16[576,768]{1,0:T(8,128)(2,1)}, u32[]{:S(2)}, u32[]{:S(2)}) collective-permute-start(bf16[576,768]{1,0:T(8,128)(2,1)} %get-tuple-element.117), channel_id=1, source_target_pairs={{0,2},{1,3},{2,0},{3,1},{4,6},{5,7},{6,4},{7,5},{8,10},{9,11},{10,... | collective-permute-start | bytes 2654216 | tf_op jit(solution)/shard_map/ppermute | solution.py:342
  60.8 57.9 %collective-permute-start.1 = (bf16[576,768]{1,0:T(8,128)(2,1)}, bf16[576,768]{1,0:T(8,128)(2,1)S(1)}, u32[]{:S(2)}, u32[]{:S(2)}) collective-permute-start(bf16[576,768]{1,0:T(8,128)(2,1)} %get-tuple-element.117), channel_id=1, source_target_pairs={{0,4},{1,5},{2,6},{3,7},{4,0},{5,1},{6,2},{7,3},{8,12},{9,13},{10,... | collective-permute-start | bytes 2654216 | tf_op jit(solution)/shard_map/ppermute | solution.py:342
  117.0 31.6 %copy-start.11 = (bf16[768,576]{1,0:T(8,128)(2,1)}, bf16[768,576]{1,0:T(8,128)(2,1)S(1)}, u32[]{:S(2)}) copy-start(bf16[768,576]{1,0:T(8,128)(2,1)S(1)} %all_gather.9) | copy-start | bytes 2654212
  117.0 25.8 %collective-permute-start.4 = (bf16[576,768]{1,0:T(8,128)(2,1)}, bf16[576,768]{1,0:T(8,128)(2,1)}, u32[]{:S(2)}, u32[]{:S(2)}) collective-permute-start(bf16[576,768]{1,0:T(8,128)(2,1)} %get-tuple-element.117), channel_id=1, source_target_pairs={{0,1},{1,0},{2,3},{3,2},{4,5},{5,4},{6,7},{7,6},{8,9},{9,8},{10,11... | collective-permute-start | bytes 2654216 | tf_op jit(solution)/shard_map/ppermute | solution.py:342
  118.6 22.1 %collective-permute-start.2 = (bf16[288,768]{1,0:T(8,128)(2,1)S(1)}, bf16[288,768]{1,0:T(8,128)(2,1)S(1)}, u32[]{:S(2)}, u32[]{:S(2)}) collective-permute-start(bf16[288,768]{1,0:T(8,128)(2,1)S(1)} %slice.255), channel_id=1, source_target_pairs={{0,4},{1,5},{2,6},{3,7},{4,0},{5,1},{6,2},{7,3},{8,12},{9,13},{10,... | collective-permute-start | bytes 1327112 | tf_op jit(solution)/shard_map/ppermute | solution.py:342
  118.8 22.8 %collective-permute-start.3 = (bf16[288,768]{1,0:T(8,128)(2,1)S(1)}, bf16[288,768]{1,0:T(8,128)(2,1)S(1)}, u32[]{:S(2)}, u32[]{:S(2)}) collective-permute-start(bf16[288,768]{1,0:T(8,128)(2,1)S(1)} %slice.256), channel_id=1, source_target_pairs={{0,2},{1,3},{2,0},{3,1},{4,6},{5,7},{6,4},{7,5},{8,10},{9,11},{10,... | collective-permute-start | bytes 1327112 | tf_op jit(solution)/shard_map/ppermute | solution.py:342
  120.4 24.6 %collective-permute-start.5 = (bf16[576,768]{1,0:T(8,128)(2,1)}, bf16[576,768]{1,0:T(8,128)(2,1)S(1)}, u32[]{:S(2)}, u32[]{:S(2)}) collective-permute-start(bf16[576,768]{1,0:T(8,128)(2,1)} %collective-permute-done), channel_id=1, source_target_pairs={{0,1},{1,0},{2,3},{3,2},{4,5},{5,4},{6,7},{7,6},{8,9},{9,8},{10,11... | collective-permute-start | bytes 2654216 | tf_op jit(solution)/shard_map/ppermute | solution.py:342
  120.6 25.4 %collective-permute-start.6 = (bf16[576,768]{1,0:T(8,128)(2,1)S(1)}, bf16[576,768]{1,0:T(8,128)(2,1)S(1)}, u32[]{:S(2)}, u32[]{:S(2)}) collective-permute-start(bf16[576,768]{1,0:T(8,128)(2,1)S(1)} %collective-permute-done.1), channel_id=1, source_target_pairs={{0,1},{1,0},{2,3},{3,2},{4,5},{5,4},{6,7},{7,6},{8,9},{9,8},{10,11... | collective-permute-start | bytes 2654216 | tf_op jit(solution)/shard_map/ppermute | solution.py:342
  140.7 6.3 %collective-permute-start.7 = (bf16[288,768]{1,0:T(8,128)(2,1)S(1)}, bf16[288,768]{1,0:T(8,128)(2,1)S(1)}, u32[]{:S(2)}, u32[]{:S(2)}) collective-permute-start(bf16[288,768]{1,0:T(8,128)(2,1)S(1)} %collective-permute-done.2), channel_id=1, source_target_pairs={{0,1},{1,0},{2,3},{3,2},{4,5},{5,4},{6,7},{7,6},{8,9},{9,8},{10,11... | collective-permute-start | bytes 1327112 | tf_op jit(solution)/shard_map/ppermute | solution.py:342
  141.6 6.2 %collective-permute-start.8 = (bf16[288,768]{1,0:T(8,128)(2,1)S(1)}, bf16[288,768]{1,0:T(8,128)(2,1)S(1)}, u32[]{:S(2)}, u32[]{:S(2)}) collective-permute-start(bf16[288,768]{1,0:T(8,128)(2,1)S(1)} %collective-permute-done.3), channel_id=1, source_target_pairs={{0,1},{1,0},{2,3},{3,2},{4,5},{5,4},{6,7},{7,6},{8,9},{9,8},{10,11... | collective-permute-start | bytes 1327112 | tf_op jit(solution)/shard_map/ppermute | solution.py:342
  215.5 21.9 %all-to-all-start.3 = ((bf16[8,144,384]{2,1,0:T(8,128)(2,1)}), bf16[8,144,384]{2,1,0:T(8,128)(2,1)S(1)}, u32[]{:S(2)}, u32[]{:S(2)}) async-start(bf16[8,144,384]{2,1,0:T(8,128)(2,1)} %reshape_reshape.20), calls=%async_computation.3 | async-start | bytes 1769472 | tf_op jit(solution)/shard_map/all_to_all | solution.py:454
  237.4 23.6 %all-to-all-start.2 = ((bf16[4,144,768]{2,1,0:T(8,128)(2,1)}), bf16[4,144,768]{2,1,0:T(8,128)(2,1)S(1)}, u32[]{:S(2)}, u32[]{:S(2)}) async-start(bf16[4,144,768]{2,1,0:T(8,128)(2,1)} %param.21), calls=%async_computation.2 | async-start | bytes 1769472 | tf_op jit(solution)/shard_map/all_to_all | solution.py:475
  241.3 315.5 %all-gather.5.cloned.1.call-start = ((), (), s32[]{:S(2)}) async-start(), calls=%async_computation.12 | async-start | bytes 4915200 | tf_op jit(solution)/shard_map/all_gather | solution.py:489
  327.9 26.5 %all-to-all-start.5 = ((bf16[4,144,768]{2,1,0:T(8,128)(2,1)}), bf16[4,144,768]{2,1,0:T(8,128)(2,1)}, u32[]{:S(2)}, u32[]{:S(2)}) async-start(bf16[4,144,768]{2,1,0:T(8,128)(2,1)} %bitcast.58), calls=%async_computation.5 | async-start | bytes 1769472 | tf_op jit(solution)/shard_map/all_to_all | solution.py:499
  332.2 270.7 %reduce-scatter.2.cloned.1.call-start = ((), (), s32[]{:S(2)}) async-start(), calls=%async_computation.13 | async-start | bytes 11354112 | tf_op jit(solution)/shard_map/reduce_scatter | solution.py:507
  447.6 46.2 %all-to-all-start.7 = ((bf16[8,96,576]{2,1,0:T(8,128)(2,1)}), bf16[8,96,576]{2,1,0:T(8,128)(2,1)}, u32[]{:S(2)}, u32[]{:S(2)}) async-start(bf16[8,96,576]{2,1,0:T(8,128)(2,1)} %pad_maximum_fusion.2), calls=%async_computation.7 | async-start | bytes 1966080 | tf_op jit(solution)/shard_map/all_to_all | solution.py:522
  469.3 29.8 %copy-start.27 = (f32[768]{0:T(1024)S(1)}, f32[768]{0:T(1024)}, u32[]{:S(2)}) copy-start(f32[768]{0:T(1024)} %get-tuple-element.100) | copy-start | bytes 9220
  469.3 29.9 %copy-start.29 = (f32[4,1,768]{2,1,0:T(1,128)S(1)}, f32[4,1,768]{2,1,0:T(1,128)}, u32[]{:S(2)}) copy-start(f32[4,1,768]{2,1,0:T(1,128)} %get-tuple-element.48) | copy-start | bytes 36868
  493.8 56.3 %all-to-all-start.6 = ((bf16[8,720,384]{2,1,0:T(8,128)(2,1)}), bf16[8,720,384]{2,1,0:T(8,128)(2,1)}, u32[]{:S(2)}, u32[]{:S(2)}) async-start(bf16[8,720,384]{2,1,0:T(8,128)(2,1)} %pad_maximum_fusion.1), calls=%async_computation.6 | async-start | bytes 8847360 | tf_op jit(solution)/shard_map/all_to_all | solution.py:454
  565.9 10.8 %all-to-all-start.9 = ((f32[32,8,128]{2,1,0:T(8,128)}), f32[32,8,128]{2,1,0:T(8,128)S(1)}, u32[]{:S(2)}, u32[]{:S(2)}) async-start(f32[32,8,128]{2,1,0:T(8,128)} %bitcast.110), calls=%async_computation.9 | async-start | bytes 262144 | tf_op jit(solution)/shard_map/all_to_all | solution.py:555
  576.6 26.2 %all-to-all-start.8 = ((bf16[4,144,768]{2,1,0:T(8,128)(2,1)}), bf16[4,144,768]{2,1,0:T(8,128)(2,1)S(1)}, u32[]{:S(2)}, u32[]{:S(2)}) async-start(bf16[4,144,768]{2,1,0:T(8,128)(2,1)} %bitcast.80), calls=%async_computation.8 | async-start | bytes 1769472 | tf_op jit(solution)/shard_map/all_to_all | solution.py:532
  (30 other events, 198.6 us)
Sparse Core Ops, SparseCore 0:
  51.1 103.7 all-gather.2
  246.1 32.4 all-gather.4
  354.6 157.4 reduce-scatter.1
